TPU v7x, 32 devices: a whole 2x2x4 slice. The times are simulated.
32 devices in a mesh: tm: 4 (over x, core), rows: 8 (over z, y).
Axes of the slice: x: 2, y: 2, z: 4, core: 2. Of those that a mesh axis runs over, the one named last changes fastest.
Arguments:
- latent: bfloat16 [16, 192, 32, 128], P('tm', None, 'rows'), may hold values from -6 to 6
- clip_ids: int32 [16], replicated, may hold values from 0 to 1, as said below
- gain_in: float32 [192], replicated, may hold values from 0.1 to 1.9
- conv_in: bfloat16 [3, 3, 3, 96, 192], replicated, may hold values from -0.078125 to 0.078125
- bias_in: float32 [96], replicated, may hold values from -3 to 3
- gain_mid: float32 [96], replicated, may hold values from 0.1 to 1.9
- conv_mid: bfloat16 [3, 3, 3, 96, 96], replicated, may hold values from -0.125 to 0.125
- bias_mid: float32 [96], replicated, may hold values from -3 to 3
- skip_weight: bfloat16 [96, 192], replicated, may hold values from -0.4375 to 0.4375
- skip_bias: float32 [96], replicated, may hold values from -3 to 3
Outputs:
- decoded: bfloat16 [16, 96, 32, 128], P('tm', None, 'rows')
Inputs may be any that keep to these rules, and one draw needn't show every extreme that they name: `clip_ids`: clip number of each frame; numbers never fall along the frames and every number appears; each clip lies on consecutive frames, and every clip other than the window's first and last holds 1 + 4 k frames, at most 21.
All inputs are finite; a program needn't handle non-finite values.
Results may differ from a plain program's by a relative error of at most 0.0075.
Values may be sent and summed in bfloat16 or wider, within the bound.
No kernel may reach another device: no remote copies, remote signals or barrier semaphores. Data moves between devices by JAX's collectives and lax.ppermute only.
A program may use at most 64 MiB of HBM per device.

v0:
```python
import jax
import jax.numpy as jnp
from jax import lax
from jax.sharding import PartitionSpec as P


def passed_along(block, axis, distance):
    devices = range(lax.axis_size(axis))
    route = [(i - distance, i) for i in devices if i - distance in devices]
    return lax.ppermute(block, axis, route)


def padded_2(shard, sides, width):
    for axis, dim in sides:
        size, length = (lax.axis_size(axis), shard.shape[dim])
        up = [(i, (i + 1) % size) for i in range(size - 1)]
        down = [(j, i) for i, j in up]
        last = lax.slice_in_dim(shard, length - width, length, axis=dim)
        first = lax.slice_in_dim(shard, 0, width, axis=dim)
        before = lax.ppermute(last, axis, up)
        after = lax.ppermute(first, axis, down)
        shard = jnp.concatenate([before, shard, after], axis=dim)
    return shard


def keep_table(clip_ids, start, count):
    frames = start + jnp.arange(count, dtype=jnp.int32)
    final_index = clip_ids.shape[0] - 1
    own_clip = jnp.take(clip_ids, jnp.clip(frames, 0, final_index))
    tables = []
    for back_step in range(3):
        source = frames - back_step
        src_clip = jnp.take(clip_ids, jnp.clip(source, 0, final_index))
        tables.append(((source >= 0) & (src_clip == own_clip)).astype(jnp.float32))
    return jnp.stack(tables)


def norm_silu(values, gain):
    floats = values.astype(jnp.float32)
    mean_sq = jnp.mean(floats * floats, axis=1, keepdims=True)
    scaled = floats * lax.rsqrt(mean_sq + 1e-06) * gain[None, :, None, None]
    return jax.nn.silu(scaled).astype(jnp.bfloat16)


def causal_conv(padded, weight, keep, out_frames):
    total = None
    for t_tap in range(3):
        slab = padded[t_tap : t_tap + out_frames]
        part = lax.conv_general_dilated(
            slab,
            weight[t_tap],
            (1, 1),
            ((0, 0), (1, 1)),
            dimension_numbers=("NCHW", "HWOI", "NCHW"),
            preferred_element_type=jnp.float32,
        )
        term = part * keep[2 - t_tap][:, None, None, None]
        total = term if total is None else total + term
    return total


def shards(
    latent,
    clip_ids,
    gain_in,
    conv_in,
    bias_in,
    gain_mid,
    conv_mid,
    bias_mid,
    skip_weight,
    skip_bias,
):
    frames_dev = latent.shape[0]
    start = lax.axis_index("tm") * frames_dev
    keep_own = keep_table(clip_ids, start, frames_dev)
    first = norm_silu(latent, gain_in)
    earlier = passed_along(first[frames_dev - 2 :], "tm", 1)
    extended = jnp.concatenate([earlier, first], axis=0)
    extended = padded_2(extended, (("rows", 2),), 1)
    hidden = causal_conv(extended, conv_in, keep_own, frames_dev)
    hidden = (hidden + bias_in[None, :, None, None]).astype(jnp.bfloat16)
    second = norm_silu(hidden, gain_mid)
    earlier_mid = passed_along(second[frames_dev - 2 :], "tm", 1)
    extended_mid = jnp.concatenate([earlier_mid, second], axis=0)
    extended_mid = padded_2(extended_mid, (("rows", 2),), 1)
    tail = causal_conv(extended_mid, conv_mid, keep_own, frames_dev)
    short = jnp.einsum("oc,fcrw->forw", skip_weight, latent, preferred_element_type=jnp.float32)
    result = tail + bias_mid[None, :, None, None] + short + skip_bias[None, :, None, None]
    return result.astype(jnp.bfloat16)


def solution(mesh):
    return jax.shard_map(
        shards,
        mesh=mesh,
        in_specs=(P("tm", None, "rows", None), P(), P(), P(), P(), P(), P(), P(), P(), P()),
        out_specs=P("tm", None, "rows", None),
        check_vma=False,
    )
```

profile of v0, /device:TPU:25, one launch (start us, length us, event | category | flops | bytes accessed | tf_op | source)
XLA Modules:
  0.0 97.7 jit_solution(234214162559814164)
XLA Ops:
  0.0 1.3 %fusion.18 = f32[4,4,128]{2,1,0:T(4,128)S(1)} fusion(bf16[4,192,4,128]{3,2,1,0:T(4,128)(2,1)} %param.12), kind=kLoop, calls=%fused_computation.26 | loop fusion | flops 1177600 | bytes 794624 | tf_op jit(solution)/shard_map/reduce_sum | solution.py:40
  1.3 1.7 %fusion.25 = bf16[4,192,4,128]{3,1,2,0:T(8,128)(2,1)S(1)} fusion(f32[192]{0:T(256)} %param.14, f32[4,4,128]{2,1,0:T(4,128)S(1)} %add_rsqrt_fusion.1, bf16[4,192,4,128]{3,2,1,0:T(4,128)(2,1)} %param.12), kind=kLoop, calls=%fused_computation.33 | loop fusion | flops 3145728 | bytes 1581824 | tf_op jit(solution)/shard_map/convert_element_type | solution.py:42
  3.1 3.7 %collective-permute-start = (bf16[2,192,4,128]{3,1,2,0:T(8,128)(2,1)S(1)}, bf16[2,192,4,128]{3,1,2,0:T(8,128)(2,1)S(1)}, u32[]{:S(2)}, u32[]{:S(2)}) collective-permute-start(bf16[2,192,4,128]{3,1,2,0:T(8,128)(2,1)S(1)} %slice.87), channel_id=1, source_target_pairs={{0,8},{8,16},{16,24},{1,9},{9,17},{17,25},{2,10},{10,18},{18,26},{... | collective-permute-start | bytes 1179656 | tf_op jit(solution)/shard_map/ppermute | solution.py:10
  6.8 0.6 gather_fusion.1
  7.5 0.6 gather_fusion.2
  8.1 0.6 gather_fusion
  8.8 2.7 %collective-permute-done = bf16[2,192,4,128]{3,1,2,0:T(8,128)(2,1)S(1)} collective-permute-done((bf16[2,192,4,128]{3,1,2,0:T(8,128)(2,1)S(1)}, bf16[2,192,4,128]{3,1,2,0:T(8,128)(2,1)S(1)}, u32[]{:S(2)}, u32[]{:S(2)}) %collective-permute-start) | collective-permute-done | bytes 393248 | tf_op jit(solution)/shard_map/ppermute | solution.py:10
  11.5 3.1 %collective-permute-start.1 = (bf16[6,192,1,128]{3,1,2,0:T(8,128)(2,1)S(1)}, bf16[6,192,1,128]{3,1,2,0:T(8,128)(2,1)S(1)}, u32[]{:S(2)}, u32[]{:S(2)}) collective-permute-start(bf16[6,192,1,128]{3,1,2,0:T(8,128)(2,1)S(1)} %get-tuple-element.12), channel_id=1, source_target_pairs={{0,1},{1,2},{2,3},{3,4},{4,5},{5,6},{6,7},{8,9},{9,10},{10,11},{11... | collective-permute-start | bytes 884744 | tf_op jit(solution)/shard_map/ppermute | solution.py:20
  14.7 3.0 %collective-permute-start.2 = (bf16[6,192,1,128]{3,1,2,0:T(8,128)(2,1)S(1)}, bf16[6,192,1,128]{3,1,2,0:T(8,128)(2,1)S(1)}, u32[]{:S(2)}, u32[]{:S(2)}) collective-permute-start(bf16[6,192,1,128]{3,1,2,0:T(8,128)(2,1)S(1)} %get-tuple-element.13), channel_id=1, source_target_pairs={{1,0},{2,1},{3,2},{4,3},{5,4},{6,5},{7,6},{9,8},{10,9},{11,10},{12... | collective-permute-start | bytes 884744 | tf_op jit(solution)/shard_map/ppermute | solution.py:21
  17.7 2.1 %collective-permute-done.1 = bf16[6,192,1,128]{3,1,2,0:T(8,128)(2,1)S(1)} collective-permute-done((bf16[6,192,1,128]{3,1,2,0:T(8,128)(2,1)S(1)}, bf16[6,192,1,128]{3,1,2,0:T(8,128)(2,1)S(1)}, u32[]{:S(2)}, u32[]{:S(2)}) %collective-permute-start.1) | collective-permute-done | bytes 294944 | tf_op jit(solution)/shard_map/ppermute | solution.py:20
  19.9 6.0 %collective-permute-done.2 = bf16[6,192,1,128]{3,1,2,0:T(8,128)(2,1)S(1)} collective-permute-done((bf16[6,192,1,128]{3,1,2,0:T(8,128)(2,1)S(1)}, bf16[6,192,1,128]{3,1,2,0:T(8,128)(2,1)S(1)}, u32[]{:S(2)}, u32[]{:S(2)}) %collective-permute-start.2) | collective-permute-done | bytes 294944 | tf_op jit(solution)/shard_map/ppermute | solution.py:21
  26.1 2.2 %slice_bitcast_fusion = (bf16[192,6,4,128]{3,0,1,2:T(8,128)(2,1)S(1)}, bf16[192,6,4,128]{3,0,1,2:T(8,128)(2,1)}, bf16[192,6,4,128]{3,0,1,2:T(8,128)(2,1)}) fusion(bf16[6,192,6,128]{3,1,2,0:T(8,128)(2,1)S(1)} %pad_maximum_fusion), kind=kLoop, calls=%fused_computation.59 | loop fusion | bytes 7077888 | tf_op jit(solution)/shard_map/slice | solution.py:48
  28.3 2.6 %copy.72 = bf16[192,6,4,128]{0,2,3,1:T(4,128)(2,1)S(1)} copy(bf16[192,6,4,128]{3,0,1,2:T(8,128)(2,1)} %get-tuple-element.7) | data formatting | bytes 2359296
  31.0 0.7 pad.2.clone
  31.8 1.9 %fusion.4 = bf16[192,6,4,8,19]{0,2,4,3,1:T(4,128)(2,1)} fusion(bf16[192,6,4,7,2]{0,2,4,3,1:T(4,128)(2,1)S(1)} %slice.91, bf16[192,6,4,8,17]{0,2,4,3,1:T(4,128)(2,1)S(1)} %bitcast.113), kind=kLoop, calls=%fused_computation.10 | loop fusion | flops 4202496 | bytes 2783232 | tf_op jit(solution)/shard_map/conv_general_dilated | solution.py:49
  33.7 2.6 %copy.71 = bf16[192,6,4,128]{0,2,3,1:T(4,128)(2,1)S(1)} copy(bf16[192,6,4,128]{3,0,1,2:T(8,128)(2,1)} %get-tuple-element.8) | data formatting | bytes 2359296
  36.3 0.7 pad.clone
  37.1 1.9 %fusion.3 = bf16[192,6,4,8,19]{0,2,4,3,1:T(4,128)(2,1)} fusion(bf16[192,6,4,7,2]{0,2,4,3,1:T(4,128)(2,1)S(1)} %slice.89, bf16[192,6,4,8,17]{0,2,4,3,1:T(4,128)(2,1)S(1)} %bitcast.115), kind=kLoop, calls=%fused_computation.9 | loop fusion | flops 4202496 | bytes 2783232 | tf_op jit(solution)/shard_map/conv_general_dilated | solution.py:49
  39.0 1.0 %copy.73 = bf16[192,6,4,128]{0,2,3,1:T(4,128)(2,1)S(1)} copy(bf16[192,6,4,128]{3,0,1,2:T(8,128)(2,1)S(1)} %get-tuple-element.6) | data formatting | bytes 2359296
  40.0 0.7 pad.4.clone
  40.8 1.1 %fusion.5 = bf16[192,6,4,8,19]{0,2,4,3,1:T(4,128)(2,1)S(1)} fusion(bf16[192,6,4,7,2]{0,2,4,3,1:T(4,128)(2,1)S(1)} %slice.93, bf16[192,6,4,8,17]{0,2,4,3,1:T(4,128)(2,1)S(1)} %bitcast.117), kind=kLoop, calls=%fused_computation.11 | loop fusion | flops 4202496 | bytes 2783232 | tf_op jit(solution)/shard_map/conv_general_dilated | solution.py:49
  42.7 2.9 %fusion.44 = f32[4,32,17,96]{3,1,2,0:T(8,128)S(1)} fusion(bf16[192,6,4,8,19]{0,2,4,3,1:T(4,128)(2,1)S(1)} %copy-done.3, f32[4,32,17,96]{3,0,2,1:T(4,128)S(1)} %bitcast.126, pred[32,17]{0,1:T(8,128)(4,1)S(1)} %copy-done.13, bf16[3,3,3,96,192]{4,3,2,1,0:T(8,128)(2,1)S(1)} %copy-done.9), kind=kOutput, calls=%fused_computation.48 | convolution fusion | flops 722362368 | bytes 4262912 | tf_op jit(solution)/shard_map/conv_general_dilated | solution.py:49
  45.9 3.0 %fusion.38 = f32[4,32,17,96]{3,1,2,0:T(8,128)S(1)} fusion(f32[4,32,17,96]{3,1,2,0:T(8,128)S(1)} %fusion.44, bf16[192,6,4,8,19]{0,2,4,3,1:T(4,128)(2,1)S(1)} %copy-done.4, f32[4,32,17,96]{3,0,2,1:T(4,128)S(1)} %bitcast.128, pred[32,17]{0,1:T(8,128)(4,1)S(1)} %copy-done.13, bf16[3,3,3,96,192]{4,3,2,1,0:T(8,128)(2,1)S(1)} %copy-done.9), kind=kOutput, calls=%fused_computation.46 | convolution fusion | flops 722571264 | bytes 5377024 | tf_op jit(solution)/shard_map/conv_general_dilated | solution.py:49
  49.1 3.0 %multiply_reduce_fusion = (f32[4,32,17]{1,2,0:T(8,128)S(1)}, f32[4,32,17,96]{3,1,2,0:T(8,128)S(1)}) fusion(f32[96]{0:T(128)S(1)} %copy-done.11, f32[4,32,17,96]{3,1,2,0:T(8,128)S(1)} %fusion.38, f32[4,32,17,96]{3,0,2,1:T(4,128)S(1)} %bitcast.130, bf16[3,3,3,96,192]{4,3,2,1,0:T(8,128)(2,1)S(1)} %copy-done.9, bf16[192,6,4,8,19]{0,2,4,3,1:T(4,128)(2,1)S(1)} %fusion.5, ...), kind=kOutput, calls=%fused_computation.62 | convolution fusion | flops 723613568 | bytes 5386240 | tf_op jit(solution)/shard_map/conv_general_dilated | solution.py:49
  52.1 0.7 copy.53
  53.1 0.9 copy.55
  53.9 1.6 %fusion.70 = bf16[4,96,4,128]{1,2,3,0:T(4,128)(2,1)S(1)} fusion(f32[4,4,136,96]{3,0,2,1:T(4,128)S(1)} %bitcast.118, f32[96]{0:T(128)S(1)} %copy-done.8, f32[4,4,128]{1,2,0:T(8,128)} %copy.55), kind=kLoop, calls=%fused_computation.70 | loop fusion | flops 1376256 | bytes 1188224 | tf_op jit(solution)/shard_map/convert_element_type | solution.py:42
  55.7 2.7 %collective-permute-start.3 = (bf16[2,96,4,128]{1,2,3,0:T(4,128)(2,1)S(1)}, bf16[2,96,4,128]{1,2,3,0:T(4,128)(2,1)S(1)}, u32[]{:S(2)}, u32[]{:S(2)}) collective-permute-start(bf16[2,96,4,128]{1,2,3,0:T(4,128)(2,1)S(1)} %slice.96), channel_id=1, source_target_pairs={{0,8},{8,16},{16,24},{1,9},{9,17},{17,25},{2,10},{10,18},{18,26},{... | collective-permute-start | bytes 589832 | tf_op jit(solution)/shard_map/ppermute | solution.py:10
  58.4 3.3 %collective-permute-done.3 = bf16[2,96,4,128]{1,2,3,0:T(4,128)(2,1)S(1)} collective-permute-done((bf16[2,96,4,128]{1,2,3,0:T(4,128)(2,1)S(1)}, bf16[2,96,4,128]{1,2,3,0:T(4,128)(2,1)S(1)}, u32[]{:S(2)}, u32[]{:S(2)}) %collective-permute-start.3) | collective-permute-done | bytes 196640 | tf_op jit(solution)/shard_map/ppermute | solution.py:10
  61.7 0.8 fusion.87
  62.5 1.9 %collective-permute-start.4 = (bf16[6,96,1,128]{1,2,3,0:T(2,128)(2,1)S(1)}, bf16[6,96,1,128]{1,2,3,0:T(2,128)(2,1)S(1)}, u32[]{:S(2)}, u32[]{:S(2)}) collective-permute-start(bf16[6,96,1,128]{1,2,3,0:T(2,128)(2,1)S(1)} %get-tuple-element.14), channel_id=1, source_target_pairs={{0,1},{1,2},{2,3},{3,4},{4,5},{5,6},{6,7},{8,9},{9,10},{10,11},{11... | collective-permute-start | bytes 442376 | tf_op jit(solution)/shard_map/ppermute | solution.py:20
  64.4 4.5 %collective-permute-start.5 = (bf16[6,96,1,128]{1,2,3,0:T(2,128)(2,1)S(1)}, bf16[6,96,1,128]{1,2,3,0:T(2,128)(2,1)S(1)}, u32[]{:S(2)}, u32[]{:S(2)}) collective-permute-start(bf16[6,96,1,128]{1,2,3,0:T(2,128)(2,1)S(1)} %get-tuple-element.15), channel_id=1, source_target_pairs={{1,0},{2,1},{3,2},{4,3},{5,4},{6,5},{7,6},{9,8},{10,9},{11,10},{12... | collective-permute-start | bytes 442376 | tf_op jit(solution)/shard_map/ppermute | solution.py:21
  68.9 5.3 %collective-permute-done.4 = bf16[6,96,1,128]{1,2,3,0:T(2,128)(2,1)S(1)} collective-permute-done((bf16[6,96,1,128]{1,2,3,0:T(2,128)(2,1)S(1)}, bf16[6,96,1,128]{1,2,3,0:T(2,128)(2,1)S(1)}, u32[]{:S(2)}, u32[]{:S(2)}) %collective-permute-start.4) | collective-permute-done | bytes 147488 | tf_op jit(solution)/shard_map/ppermute | solution.py:20
  74.2 8.5 %collective-permute-done.5 = bf16[6,96,1,128]{1,2,3,0:T(2,128)(2,1)S(1)} collective-permute-done((bf16[6,96,1,128]{1,2,3,0:T(2,128)(2,1)S(1)}, bf16[6,96,1,128]{1,2,3,0:T(2,128)(2,1)S(1)}, u32[]{:S(2)}, u32[]{:S(2)}) %collective-permute-start.5) | collective-permute-done | bytes 147488 | tf_op jit(solution)/shard_map/ppermute | solution.py:21
  82.8 1.6 %pad_maximum_fusion.1 = bf16[6,96,6,128]{1,2,3,0:T(8,128)(2,1)S(1)} fusion(bf16[6,96,1,128]{1,2,3,0:T(2,128)(2,1)S(1)} %collective-permute-done.5, bf16[4,96,4,128]{1,2,3,0:T(4,128)(2,1)S(1)} %fusion.70, bf16[2,96,4,128]{1,2,3,0:T(4,128)(2,1)S(1)} %collective-permute-done.3, bf16[6,96,1,128]{1,2,3,0:T(2,128)(2,1)S(1)} %collective-permute-done.4), kind=kLoop, calls=%fused_computation.34 | loop fusion | flops 3538944 | bytes 1769472 | tf_op jit(solution)/shard_map/concatenate | solution.py:22
  84.4 0.5 slice_bitcast_fusion.3
  84.9 0.6 copy.76
  86.0 0.5 fusion.73
  86.5 0.6 copy.74
  87.6 0.5 fusion.71
  88.1 0.6 copy.75
  89.2 0.5 fusion.72
  89.8 1.5 %fusion.28 = f32[4,32,17,96]{3,1,2,0:T(8,128)S(1)} fusion(f32[4,32,17,96]{3,0,2,1:T(4,128)S(1)} %bitcast.127, bf16[96,6,4,8,19]{0,2,4,3,1:T(4,128)(2,1)S(1)} %fusion.72, pred[32,17]{0,1:T(8,128)(4,1)S(1)} %copy-done.13, bf16[3,3,3,96,96]{4,3,2,1,0:T(8,128)(2,1)S(1)} %copy-done.10), kind=kOutput, calls=%fused_computation.40 | convolution fusion | flops 361390080 | bytes 3107840 | tf_op jit(solution)/shard_map/conv_general_dilated | solution.py:49
  91.4 1.6 %fusion.27 = f32[4,32,17,96]{3,1,2,0:T(8,128)S(1)} fusion(f32[4,32,17,96]{3,1,2,0:T(8,128)S(1)} %fusion.28, f32[4,32,17,96]{3,0,2,1:T(4,128)S(1)} %bitcast.129, bf16[96,6,4,8,19]{0,2,4,3,1:T(4,128)(2,1)S(1)} %fusion.71, pred[32,17]{0,1:T(8,128)(4,1)S(1)} %copy-done.13, bf16[3,3,3,96,96]{4,3,2,1,0:T(8,128)(2,1)S(1)} %copy-done.10), kind=kOutput, calls=%fused_computation.39 | convolution fusion | flops 361598976 | bytes 4221952 | tf_op jit(solution)/shard_map/conv_general_dilated | solution.py:49
  93.0 1.6 %fusion.31 = f32[4,32,17,96]{3,1,2,0:T(8,128)S(1)} fusion(f32[4,32,17,96]{3,1,2,0:T(8,128)S(1)} %fusion.27, f32[4,32,17,96]{3,0,2,1:T(4,128)S(1)} %bitcast.131, bf16[96,6,4,8,19]{0,2,4,3,1:T(4,128)(2,1)S(1)} %fusion.73, f32[96]{0:T(128)S(1)} %copy-done.12, pred[32,17]{0,1:T(8,128)(4,1)S(1)} %copy-done.13, bf16[3,3,3,96,96]{4,3,2,1,0:T(8,128)(2,1)S(1)} %copy-done.10), kind=kOutput, calls=%fused_computation.43 | convolution fusion | flops 361807872 | bytes 4222464 | tf_op jit(solution)/shard_map/conv_general_dilated | solution.py:49
  94.6 0.7 copy.65
  95.7 0.7 copy-done.2
  96.7 0.9 copy.68
  (58 shorter events, 4.2 us)
Async XLA Ops:
  0.0 95.7 %copy-start = (bf16[96,192]{1,0:T(8,128)(2,1)S(1)}, bf16[96,192]{1,0:T(8,128)(2,1)}, u32[]{:S(2)}) copy-start(bf16[96,192]{1,0:T(8,128)(2,1)} %param.20) | copy-start | bytes 110596
  0.0 6.8 %copy-start.1 = (s32[16]{0:T(128)S(1)}, s32[16]{0:T(128)}, u32[]{:S(2)}) copy-start(s32[16]{0:T(128)} %param.13) | copy-start | bytes 196
  3.1 8.4 %collective-permute-start = (bf16[2,192,4,128]{3,1,2,0:T(8,128)(2,1)S(1)}, bf16[2,192,4,128]{3,1,2,0:T(8,128)(2,1)S(1)}, u32[]{:S(2)}, u32[]{:S(2)}) collective-permute-start(bf16[2,192,4,128]{3,1,2,0:T(8,128)(2,1)S(1)} %slice.87), channel_id=1, source_target_pairs={{0,8},{8,16},{16,24},{1,9},{9,17},{17,25},{2,10},{10,18},{18,26},{... | collective-permute-start | bytes 1179656 | tf_op jit(solution)/shard_map/ppermute | solution.py:10
  11.5 8.4 %collective-permute-start.1 = (bf16[6,192,1,128]{3,1,2,0:T(8,128)(2,1)S(1)}, bf16[6,192,1,128]{3,1,2,0:T(8,128)(2,1)S(1)}, u32[]{:S(2)}, u32[]{:S(2)}) collective-permute-start(bf16[6,192,1,128]{3,1,2,0:T(8,128)(2,1)S(1)} %get-tuple-element.12), channel_id=1, source_target_pairs={{0,1},{1,2},{2,3},{3,4},{4,5},{5,6},{6,7},{8,9},{9,10},{10,11},{11... | collective-permute-start | bytes 884744 | tf_op jit(solution)/shard_map/ppermute | solution.py:20
  14.7 11.2 %collective-permute-start.2 = (bf16[6,192,1,128]{3,1,2,0:T(8,128)(2,1)S(1)}, bf16[6,192,1,128]{3,1,2,0:T(8,128)(2,1)S(1)}, u32[]{:S(2)}, u32[]{:S(2)}) collective-permute-start(bf16[6,192,1,128]{3,1,2,0:T(8,128)(2,1)S(1)} %get-tuple-element.13), channel_id=1, source_target_pairs={{1,0},{2,1},{3,2},{4,3},{5,4},{6,5},{7,6},{9,8},{10,9},{11,10},{12... | collective-permute-start | bytes 884744 | tf_op jit(solution)/shard_map/ppermute | solution.py:21
  40.8 1.5 %copy-start.3 = (bf16[192,6,4,8,19]{0,2,4,3,1:T(4,128)(2,1)S(1)}, bf16[192,6,4,8,19]{0,2,4,3,1:T(4,128)(2,1)}, u32[]{:S(2)}) copy-start(bf16[192,6,4,8,19]{0,2,4,3,1:T(4,128)(2,1)} %fusion.4) | copy-start | bytes 4202500
  40.8 1.9 %copy-start.9 = (bf16[3,3,3,96,192]{4,3,2,1,0:T(8,128)(2,1)S(1)}, bf16[3,3,3,96,192]{4,3,2,1,0:T(8,128)(2,1)}, u32[]{:S(2)}) copy-start(bf16[3,3,3,96,192]{4,3,2,1,0:T(8,128)(2,1)} %param.15) | copy-start | bytes 2985988
  40.8 1.9 %copy-start.13 = (pred[32,17]{0,1:T(8,128)(4,1)S(1)}, pred[32,17]{0,1:T(8,128)(4,1)}, u32[]{:S(2)}) copy-start(pred[32,17]{0,1:T(8,128)(4,1)} %constant.69) | copy-start | bytes 1636
  42.7 3.1 %copy-start.4 = (bf16[192,6,4,8,19]{0,2,4,3,1:T(4,128)(2,1)S(1)}, bf16[192,6,4,8,19]{0,2,4,3,1:T(4,128)(2,1)}, u32[]{:S(2)}) copy-start(bf16[192,6,4,8,19]{0,2,4,3,1:T(4,128)(2,1)} %fusion.3) | copy-start | bytes 4202500
  45.9 3.2 %copy-start.11 = (f32[96]{0:T(128)S(1)}, f32[96]{0:T(128)}, u32[]{:S(2)}) copy-start(f32[96]{0:T(128)} %param.16) | copy-start | bytes 1156
  49.1 3.0 %copy-start.5 = (f32[4,4,136,96]{3,0,2,1:T(4,128)}, f32[4,4,136,96]{3,0,2,1:T(4,128)S(1)}, u32[]{:S(2)}) copy-start(f32[4,4,136,96]{3,0,2,1:T(4,128)S(1)} %broadcast.83) | copy-start | bytes 2506756
  52.1 1.8 %copy-start.8 = (f32[96]{0:T(128)S(1)}, f32[96]{0:T(128)}, u32[]{:S(2)}) copy-start(f32[96]{0:T(128)} %param.17) | copy-start | bytes 1156
  55.7 6.0 %collective-permute-start.3 = (bf16[2,96,4,128]{1,2,3,0:T(4,128)(2,1)S(1)}, bf16[2,96,4,128]{1,2,3,0:T(4,128)(2,1)S(1)}, u32[]{:S(2)}, u32[]{:S(2)}) collective-permute-start(bf16[2,96,4,128]{1,2,3,0:T(4,128)(2,1)S(1)} %slice.96), channel_id=1, source_target_pairs={{0,8},{8,16},{16,24},{1,9},{9,17},{17,25},{2,10},{10,18},{18,26},{... | collective-permute-start | bytes 589832 | tf_op jit(solution)/shard_map/ppermute | solution.py:10
  62.5 11.8 %collective-permute-start.4 = (bf16[6,96,1,128]{1,2,3,0:T(2,128)(2,1)S(1)}, bf16[6,96,1,128]{1,2,3,0:T(2,128)(2,1)S(1)}, u32[]{:S(2)}, u32[]{:S(2)}) collective-permute-start(bf16[6,96,1,128]{1,2,3,0:T(2,128)(2,1)S(1)} %get-tuple-element.14), channel_id=1, source_target_pairs={{0,1},{1,2},{2,3},{3,4},{4,5},{5,6},{6,7},{8,9},{9,10},{10,11},{11... | collective-permute-start | bytes 442376 | tf_op jit(solution)/shard_map/ppermute | solution.py:20
  64.4 18.4 %collective-permute-start.5 = (bf16[6,96,1,128]{1,2,3,0:T(2,128)(2,1)S(1)}, bf16[6,96,1,128]{1,2,3,0:T(2,128)(2,1)S(1)}, u32[]{:S(2)}, u32[]{:S(2)}) collective-permute-start(bf16[6,96,1,128]{1,2,3,0:T(2,128)(2,1)S(1)} %get-tuple-element.15), channel_id=1, source_target_pairs={{1,0},{2,1},{3,2},{4,3},{5,4},{6,5},{7,6},{9,8},{10,9},{11,10},{12... | collective-permute-start | bytes 442376 | tf_op jit(solution)/shard_map/ppermute | solution.py:21
  88.7 1.1 %copy-start.10 = (bf16[3,3,3,96,96]{4,3,2,1,0:T(8,128)(2,1)S(1)}, bf16[3,3,3,96,96]{4,3,2,1,0:T(8,128)(2,1)}, u32[]{:S(2)}) copy-start(bf16[3,3,3,96,96]{4,3,2,1,0:T(8,128)(2,1)} %param.18) | copy-start | bytes 1492996
  91.3 1.6 %copy-start.6 = (f32[4,4,136,96]{3,0,2,1:T(4,128)S(1)}, f32[4,4,136,96]{3,0,2,1:T(4,128)}, u32[]{:S(2)}) copy-start(f32[4,4,136,96]{3,0,2,1:T(4,128)} %copy-done.5) | copy-start | bytes 2506756
  91.4 1.6 %copy-start.12 = (f32[96]{0:T(128)S(1)}, f32[96]{0:T(128)}, u32[]{:S(2)}) copy-start(f32[96]{0:T(128)} %param.19) | copy-start | bytes 1156
  95.3 1.1 %copy-start.2 = (bf16[4,192,4,128]{3,2,1,0:T(4,128)(2,1)S(1)}, bf16[4,192,4,128]{3,2,1,0:T(4,128)(2,1)}, u32[]{:S(2)}) copy-start(bf16[4,192,4,128]{3,2,1,0:T(4,128)(2,1)} %param.12) | copy-start | bytes 2359300
  95.3 1.1 %copy-start.7 = (f32[96]{0:T(128)S(1)}, f32[96]{0:T(128)}, u32[]{:S(2)}) copy-start(f32[96]{0:T(128)} %param.21) | copy-start | bytes 1156
where the time goes:
time: 98.1 us; the launch traced here: 97.7 us
  waiting for transfers between devices  28 us (29%)
  local copies, waits for them, and re-layouts  22.4 us (23%)
  starting transfers between devices  19 us (19%)
  matrix products  13.9 us (14%)
  other arithmetic  13.8 us (14%)
    ppermute x2, waiting for transfers between devices, padded_2(): after = lax.ppermute(first, axis, down)  14.5 us
    conv_general_dilated x6, matrix products, causal_conv(): lax.conv_general_dilated(slab, weight[t_tap], (1, 1), ((0, 0), (1, 1)), d...  13.6 us
    unnamed x35, local copies, waits for them, and re-layouts  9.8 us
    ppermute x2, starting transfers between devices, padded_2(): after = lax.ppermute(first, axis, down)  7.52 us
    ppermute x2, waiting for transfers between devices, padded_2(): before = lax.ppermute(last, axis, up)  7.48 us
    ppermute x2, starting transfers between devices, passed_along(): return lax.ppermute(block, axis, route)  6.38 us
    conv_general_dilated x6, other arithmetic, causal_conv(): lax.conv_general_dilated(slab, weight[t_tap], (1, 1), ((0, 0), (1, 1)), d...  6.36 us
    slice x8, local copies, waits for them, and re-layouts, causal_conv(): slab = padded[t_tap:t_tap + out_frames]  6.17 us
  transfers between devices with their start and end apart: 6, of which 6 were waited for; matrix products, arithmetic and copies ran while one was open for 2% of the time, Pallas kernels for 0%

commit v1 on v0

v1 whole, which is shorter than its diff:
```python
import jax
import jax.numpy as jnp
from jax import lax
from jax.experimental import pallas as pl
from jax.experimental.pallas import tpu as pltpu
from jax.sharding import PartitionSpec as P

F32 = jnp.float32
BF16 = jnp.bfloat16
VMEM = pl.BlockSpec(memory_space=pltpu.VMEM)
SMEM = pl.BlockSpec(memory_space=pltpu.SMEM)


def silu_norm(values, gain):
    mean_sq = jnp.mean(values * values, axis=0, keepdims=True)
    scaled = values * lax.rsqrt(mean_sq + 1e-06) * gain
    return scaled / (1.0 + jnp.exp(-scaled))


def column_taps(act):
    lane = lax.broadcasted_iota(jnp.int32, act.shape, 1)
    width = act.shape[1]
    left = jnp.where(lane == 0, 0.0, pltpu.roll(act, 1, 1))
    right = jnp.where(lane == width - 1, 0.0, pltpu.roll(act, width - 1, 1))
    return left.astype(BF16), act.astype(BF16), right.astype(BF16)


def spread(vector, width):
    return jnp.broadcast_to(vector, (width, vector.shape[1])).T


def kept(clip_ref, frame, back):
    final = clip_ref.shape[0] - 1
    here = clip_ref[jnp.clip(frame, 0, final)]
    there = clip_ref[jnp.clip(frame - back, 0, final)]
    return (frame - back >= 0) & (here == there)


def fold_taps(weight_ref, row_tap, first, last):
    return jnp.concatenate([weight_ref[t, row_tap, j] for t in range(first, last + 1) for j in range(3)], axis=1)


def dot(a, b):
    return jnp.dot(a, b, preferred_element_type=F32)


def by_suffix(clip_ref, frame, first, last, body, nothing):
    flags = [None if t == 2 else kept(clip_ref, frame, 2 - t) for t in range(first, last + 1)]
    prior = None
    for t, flag in zip(range(first, last + 1), flags):
        here = flag if prior is None else (~prior if flag is None else ~prior & flag)
        if here is None:
            body(t)
            return
        pl.when(here)(lambda t=t: body(t))
        prior = flag
    if last != 2:
        pl.when(~prior)(nothing)


def conv_first(xs_ref, wt_ref, wu_ref, clip_ref, start, columns, frames, emit):
    depth = xs_ref.shape[0] // frames
    for out in range(frames + 2):
        first, last = max(0, 2 - out), min(2, frames + 1 - out)

        def body(t, out=out, last=last):
            rows = pl.ds((out - 2 + t) * depth, (last + 1 - t) * depth)
            if t == 1:
                weight = wu_ref[:, : (last + 1 - t) * depth]
            else:
                weight = wt_ref[:, t * depth : (last + 1) * depth]
            emit(out, dot(weight, xs_ref[rows, columns]))

        def nothing(out=out):
            emit(out, jnp.zeros((wt_ref.shape[0], columns.size), F32))

        by_suffix(clip_ref, start + out, first, last, body, nothing)


def first_kernel(clip_ref, lat_ref, weight_ref, gain_ref, xs_ref, wt_ref, wu_ref, up_ref, edge_ref):
    frames, chans, pixels = lat_ref.shape
    outs = weight_ref.shape[3]
    width = up_ref.shape[2] // 2
    height = pixels // width
    start = lax.axis_index("tm") * frames
    gain = spread(gain_ref[...], width)
    for i in range(3):
        wt_ref[i * outs : (i + 1) * outs, :] = fold_taps(weight_ref, i, 0, 2)
        wu_ref[i * outs : (i + 1) * outs, :] = fold_taps(weight_ref, i, 1, 2)
    for f in range(frames):
        for r in range(height):
            cols = pl.ds(r * width, width)
            act = silu_norm(lat_ref[f, :, cols].astype(F32), gain)
            for j, tap in enumerate(column_taps(act)):
                xs_ref[pl.ds((f * 3 + j) * chans, chans), cols] = tap

    def emit(out, y):
        y0, y1, y2 = (y[i * outs : (i + 1) * outs] for i in range(3))
        far = y0[:, :width] + y1[:, width:]
        up_ref[out, :, :width] = far.astype(BF16)
        up_ref[out, :, width:] = y0[:, width:].astype(BF16)
        edge_ref[out, :, :width] = y2[:, :width]
        edge_ref[out, :, width : 2 * width] = y1[:, :width] + y2[:, width:]
        edge_ref[out, :, 2 * width :] = far

    conv_first(xs_ref, wt_ref, wu_ref, clip_ref, start, pl.ds(pixels - 2 * width, 2 * width), frames, emit)


def inner_kernel(clip_ref, xs_ref, wt_ref, wu_ref, edge_ref, part_ref):
    width = edge_ref.shape[2] // 3
    outs = edge_ref.shape[1]
    frames = edge_ref.shape[0] - 2
    inner = part_ref.shape[2] // width - 3
    start = lax.axis_index("tm") * frames

    def emit(out, y):
        y0, y1, y2 = (y[i * outs : (i + 1) * outs] for i in range(3))
        for h in range(-1, inner + 2):
            total = None
            for tap, row in ((y0, h - 1), (y1, h), (y2, h + 1)):
                if 0 <= row < inner:
                    term = tap[:, row * width : (row + 1) * width]
                    total = term if total is None else total + term
            if h >= inner - 1:
                e = h - inner + 1
                term = edge_ref[out, :, e * width : (e + 1) * width]
                total = term if total is None else total + term
            part_ref[out, :, (h + 1) * width : (h + 2) * width] = total

    conv_first(xs_ref, wt_ref, wu_ref, clip_ref, start, pl.ds(0, inner * width), frames, emit)


def act_rows(total, h, height, bias, gain):
    hidden = (total + bias).astype(BF16).astype(F32)
    act = silu_norm(hidden, gain)
    if h == -1:
        return jnp.where(lax.axis_index("rows") > 0, act, 0.0)
    if h == height - 1:
        return jnp.where(lax.axis_index("rows") == lax.axis_size("rows") - 1, act, 0.0)
    return act


def hidden_sum(part_ref, got_ref, out, h, width):
    total = part_ref[out, :, (h + 1) * width : (h + 2) * width]
    if h < 1:
        total = total + got_ref[out, :, (h + 1) * width : (h + 2) * width].astype(F32)
    return total


def later_kernel(part_ref, got_ref, bias_ref, gain_ref, msg_ref):
    width = got_ref.shape[2] // 2
    frames = part_ref.shape[0] - 2
    height = part_ref.shape[2] // width - 1
    bias, gain = spread(bias_ref[...], width), spread(gain_ref[...], width)
    for k in range(4):
        for h in range(-1, height):
            total = hidden_sum(part_ref, got_ref, frames - 2 + k, h, width)
            cols = pl.ds((h + 1) * width, width)
            if k < 2:
                total = act_rows(total, h, height, bias, gain)
            msg_ref[k, :, cols] = total.astype(BF16)


def conv_second(xs_ref, wt_refs, clip_ref, start, columns, frames, emit):
    depth = xs_ref.shape[0] // (frames + 2)
    for out in range(frames):

        def body(t, out=out):
            rows = pl.ds((out + t) * depth, (3 - t) * depth)
            emit(out, dot(wt_refs[t][...], xs_ref[rows, columns]))

        by_suffix(clip_ref, start + out, 0, 2, body, None)


def second_kernel(clip_ref, part_ref, got_ref, mine_ref, before_ref, weight_ref, bias_ref, gain_ref, xs_ref, w0_ref, w1_ref, w2_ref, down_ref, edge_ref):
    width = got_ref.shape[2] // 2
    frames = part_ref.shape[0] - 2
    height = part_ref.shape[2] // width - 1
    outs = part_ref.shape[1]
    start = lax.axis_index("tm") * frames
    bias, gain = spread(bias_ref[...], width), spread(gain_ref[...], width)
    refs = (w0_ref, w1_ref, w2_ref)
    for t, ref in enumerate(refs):
        for i in range(3):
            ref[i * outs : (i + 1) * outs, :] = fold_taps(weight_ref, i, t, 2)
    for s in range(-2, frames):
        for h in range(-1, height):
            cols = pl.ds((h + 1) * width, width)
            if s < 0:
                act = before_ref[s + 2, :, cols].astype(F32)
            elif s >= frames - 2:
                act = mine_ref[s - frames + 2, :, cols].astype(F32)
            else:
                total = hidden_sum(part_ref, got_ref, s, h, width)
                if s < 2:
                    total = total + before_ref[2 + s, :, cols].astype(F32)
                act = act_rows(total, h, height, bias, gain)
            for j, tap in enumerate(column_taps(act)):
                xs_ref[pl.ds(((s + 2) * 3 + j) * outs, outs), cols] = tap

    def emit(out, y):
        y0, y1, y2 = (y[i * outs : (i + 1) * outs] for i in range(3))
        down_ref[out, :, :width] = y2[:, :width].astype(BF16)
        down_ref[out, :, width:] = (y1[:, :width] + y2[:, width:]).astype(BF16)
        edge_ref[out, :, :width] = y0[:, :width] + y1[:, width:]
        edge_ref[out, :, width:] = y0[:, width:]

    conv_second(xs_ref, refs, clip_ref, start, pl.ds(0, 2 * width), frames, emit)


def last_kernel(clip_ref, xs_ref, w0_ref, w1_ref, w2_ref, edge_ref, lat_ref, skip_ref, bias_ref, skip_bias_ref, out_ref):
    width = edge_ref.shape[2] // 2
    frames, outs, pixels = out_ref.shape
    height = pixels // width
    start = lax.axis_index("tm") * frames
    bias = spread(bias_ref[...] + skip_bias_ref[...], width)
    refs = (w0_ref, w1_ref, w2_ref)
    skip = skip_ref[...]

    def emit(out, y):
        y0, y1, y2 = (y[i * outs : (i + 1) * outs] for i in range(3))
        short = dot(skip, lat_ref[out])
        for r in range(height):
            total = short[:, r * width : (r + 1) * width] + bias
            for tap, row in ((y0, r - 1), (y1, r), (y2, r + 1)):
                if 1 <= row < height:
                    total = total + tap[:, (row - 1) * width : row * width]
            if r < 2:
                total = total + edge_ref[out, :, r * width : (r + 1) * width]
            out_ref[out, :, r * width : (r + 1) * width] = total

    conv_second(xs_ref, refs, clip_ref, start, pl.ds(2 * width, (height - 1) * width), frames, emit)


def call(kernel, shapes, operands, flops, smem=0):
    moved = sum(x.size * x.dtype.itemsize for x in operands) + sum(s.size * s.dtype.itemsize for s in shapes)
    single = len(shapes) == 1
    return pl.pallas_call(
        kernel,
        out_shape=shapes[0] if single else tuple(shapes),
        in_specs=[SMEM] * smem + [VMEM] * (len(operands) - smem),
        out_specs=VMEM if single else tuple(VMEM for _ in shapes),
        cost_estimate=pl.CostEstimate(flops=flops, bytes_accessed=moved, transcendentals=0),
    )(*operands)


def moved_by(block, axis, distance):
    devices = range(lax.axis_size(axis))
    return lax.ppermute(block, axis, [(i, i + distance) for i in devices if i + distance in devices])


def shards(latent, clip_ids, gain_in, conv_in, bias_in, gain_mid, conv_mid, bias_mid, skip_weight, skip_bias):
    frames, chans, height, width = latent.shape
    outs = conv_in.shape[3]
    shape = jax.ShapeDtypeStruct
    lat = latent.reshape(frames, chans, height * width)
    row = lambda v: v.reshape(1, -1)
    deep, deep_mid, tall = 3 * chans, 3 * outs, 3 * outs
    work = 2 * tall * 3 * deep * frames * width
    xs, wt, wu, up, edge = call(
        first_kernel,
        [
            shape((frames * deep, height * width), BF16),
            shape((tall, 3 * deep), BF16),
            shape((tall, 2 * deep), BF16),
            shape((frames + 2, outs, 2 * width), BF16),
            shape((frames + 2, outs, 3 * width), F32),
        ],
        (clip_ids, lat, conv_in, row(gain_in)),
        work * 2,
        1,
    )
    got = moved_by(up, "rows", 1)
    part = call(
        inner_kernel,
        [shape((frames + 2, outs, (height + 1) * width), F32)],
        (clip_ids, xs, wt, wu, edge),
        work * (height - 2),
        1,
    )
    msg = call(
        later_kernel,
        [shape((4, outs, (height + 1) * width), BF16)],
        (part, got, row(bias_in), row(gain_mid)),
        1000,
    )
    before = moved_by(msg, "tm", 1)
    xs_mid, w0, w1, w2, down, edge_mid = call(
        second_kernel,
        [
            shape(((frames + 2) * deep_mid, (height + 1) * width), BF16),
            shape((tall, 3 * deep_mid), BF16),
            shape((tall, 2 * deep_mid), BF16),
            shape((tall, deep_mid), BF16),
            shape((frames, outs, 2 * width), BF16),
            shape((frames, outs, 2 * width), F32),
        ],
        (clip_ids, part, got, msg, before, conv_mid, row(bias_in), row(gain_mid)),
        work,
        1,
    )
    below = moved_by(down, "rows", -1)
    total = call(
        last_kernel,
        [shape((frames, outs, height * width), F32)],
        (clip_ids, xs_mid, w0, w1, w2, edge_mid, lat, skip_weight, row(bias_mid), row(skip_bias)),
        work * (height - 2) // 2,
        1,
    )
    tail = total[:, :, (height - 2) * width :] + below.astype(F32)
    result = jnp.concatenate([total[:, :, : (height - 2) * width], tail], axis=2)
    return result.astype(BF16).reshape(frames, outs, height, width)


def solution(mesh):
    return jax.shard_map(
        shards,
        mesh=mesh,
        in_specs=(P("tm", None, "rows", None), P(), P(), P(), P(), P(), P(), P(), P(), P()),
        out_specs=P("tm", None, "rows", None),
        check_vma=False,
    )
```

time: 98.1 us -> 53.2 us (0.54)
  the two profiles are of different devices: /device:TPU:25 before, /device:TPU:22 now
where the time goes in v1:
time: 53.2 us; the launch traced here: 52.9 us
  Pallas kernels  26.9 us (51%)
  waiting for transfers between devices  10.1 us (19%)
  starting transfers between devices  8.63 us (16%)
  local copies, waits for them, and re-layouts  4.97 us (9%)
  other arithmetic  2.2 us (4%)
    pallas_call x5, Pallas kernels, call(): pl.pallas_call(kernel, out_shape=shapes[0] if single else tuple(shapes),...  26.9 us
    ppermute x3, waiting for transfers between devices, moved_by(): lax.ppermute(block, axis, [(i, i + distance) for i in devices if i + dist...  10.1 us
    ppermute x3, starting transfers between devices, moved_by(): lax.ppermute(block, axis, [(i, i + distance) for i in devices if i + dist...  8.63 us
    reshape x1, local copies, waits for them, and re-layouts, shards(): lat = latent.reshape(frames, chans, height * width)  2.34 us
    unnamed x4, local copies, waits for them, and re-layouts  1.51 us
    concatenate x1, other arithmetic, shards(): result = jnp.concatenate([total[:, :, :(height - 2) * width], tail], axis=2)  1.16 us
  transfers between devices with their start and end apart: 3, of which 2 were waited for; matrix products, arithmetic and copies ran while one was open for 2% of the time, Pallas kernels for 21%

profile of v1, /device:TPU:22, one launch (start us, length us, event | category | flops | bytes accessed | tf_op | source)
XLA Modules:
  0.0 52.9 jit_solution(6467052815817758604)
XLA Ops:
  0.0 2.3 %reshape.25.lat_ref = bf16[4,192,512]{2,1,0:T(8,128)(2,1)} reshape(bf16[4,192,4,128]{3,2,1,0:T(4,128)(2,1)} %param.10) | data formatting | bytes 1572864 | tf_op jit(solution)/shard_map/reshape | solution.py:256
  2.3 7.1 %shard_map.100 = (bf16[2304,512]{1,0:T(8,128)(2,1)}, bf16[288,1728]{1,0:T(8,128)(2,1)}, bf16[288,1152]{1,0:T(8,128)(2,1)}, bf16[6,96,256]{2,1,0:T(8,128)(2,1)}, f32[6,96,384]{2,1,0:T(8,128)}) custom-call(s32[16]{0:T(128)} %clip_ref.7, bf16[4,192,512]{2,1,0:T(8,128)(2,1)} %reshape.25.lat_ref, bf16[3,3,3,96,192]{4,3,2,1,0:T(8,128)(2,1)} %weight_ref.2, ...), custom_call_target="tpu_custom_call" | custom-call | flops 1019215872 | bytes 6980416 | tf_op jit(solution)/shard_map/pallas_call | solution.py:238
  9.4 3.4 %collective-permute-start = (bf16[6,96,256]{2,1,0:T(8,128)(2,1)}, bf16[6,96,256]{2,1,0:T(8,128)(2,1)S(1)}, u32[]{:S(2)}, u32[]{:S(2)}) collective-permute-start(bf16[6,96,256]{2,1,0:T(8,128)(2,1)} %get-tuple-element.20), channel_id=1, source_target_pairs={{0,1},{1,2},{2,3},{3,4},{4,5},{5,6},{6,7},{8,9},{9,10},{10,11},{11... | collective-permute-start | bytes 884744 | tf_op jit(solution)/shard_map/ppermute | solution.py:249
  12.9 5.7 %shard_map.101.part_ref = f32[6,96,640]{2,1,0:T(8,128)} custom-call(s32[16]{0:T(128)} %clip_ref.7, bf16[2304,512]{1,0:T(8,128)(2,1)} %get-tuple-element.16.xs_ref, bf16[288,1728]{1,0:T(8,128)(2,1)} %get-tuple-element.17.wt_ref, bf16[288,1152]{1,0:T(8,128)(2,1)} %get-tuple-element.18.wu_ref, f32[6,96,384]{2,1,0:T(8,128)} %get-tuple-element.19.edge_ref), custom_call_target="tpu_custom_call" | custom-call | flops 1019215872 | bytes 6377536 | tf_op jit(solution)/shard_map/pallas_call | solution.py:238
  18.6 1.7 %collective-permute-done.got_ref = bf16[6,96,256]{2,1,0:T(8,128)(2,1)S(1)} collective-permute-done((bf16[6,96,256]{2,1,0:T(8,128)(2,1)}, bf16[6,96,256]{2,1,0:T(8,128)(2,1)S(1)}, u32[]{:S(2)}, u32[]{:S(2)}) %collective-permute-start) | collective-permute-done | bytes 294944 | tf_op jit(solution)/shard_map/ppermute | solution.py:249
  20.3 0.0 copy-start
  20.3 0.7 %copy-done = bf16[6,96,256]{2,1,0:T(8,128)(2,1)} copy-done((bf16[6,96,256]{2,1,0:T(8,128)(2,1)}, bf16[6,96,256]{2,1,0:T(8,128)(2,1)S(1)}, u32[]{:S(2)}) %copy-start) | copy-done | bytes 294936
  21.0 2.6 %shard_map.102.mine_ref = bf16[4,96,640]{2,1,0:T(8,128)(2,1)} custom-call(f32[6,96,640]{2,1,0:T(8,128)} %shard_map.101.part_ref, bf16[6,96,256]{2,1,0:T(8,128)(2,1)} %copy-done, f32[1,96]{1,0:T(1,128)} %bitcast.5, f32[1,96]{1,0:T(1,128)} %bitcast.7), custom_call_target="tpu_custom_call" | custom-call | flops 1000 | bytes 2261760 | tf_op jit(solution)/shard_map/pallas_call | solution.py:238
  23.6 1.9 %collective-permute-start.1 = (bf16[4,96,640]{2,1,0:T(8,128)(2,1)}, bf16[4,96,640]{2,1,0:T(8,128)(2,1)S(1)}, u32[]{:S(2)}, u32[]{:S(2)}) collective-permute-start(bf16[4,96,640]{2,1,0:T(8,128)(2,1)} %shard_map.102.mine_ref), channel_id=1, source_target_pairs={{0,8},{8,16},{16,24},{1,9},{9,17},{17,25},{2,10},{10,18},{18,26},{... | collective-permute-start | bytes 1474568 | tf_op jit(solution)/shard_map/ppermute | solution.py:249
  25.5 8.4 %collective-permute-done.1.before_ref = bf16[4,96,640]{2,1,0:T(8,128)(2,1)S(1)} collective-permute-done((bf16[4,96,640]{2,1,0:T(8,128)(2,1)}, bf16[4,96,640]{2,1,0:T(8,128)(2,1)S(1)}, u32[]{:S(2)}, u32[]{:S(2)}) %collective-permute-start.1) | collective-permute-done | bytes 491552 | tf_op jit(solution)/shard_map/ppermute | solution.py:249
  33.9 0.0 copy-start.1
  33.9 0.8 %copy-done.1 = bf16[4,96,640]{2,1,0:T(8,128)(2,1)} copy-done((bf16[4,96,640]{2,1,0:T(8,128)(2,1)}, bf16[4,96,640]{2,1,0:T(8,128)(2,1)S(1)}, u32[]{:S(2)}) %copy-start.1) | copy-done | bytes 491544
  34.7 6.0 %shard_map.103 = (bf16[1728,640]{1,0:T(8,128)(2,1)}, bf16[288,864]{1,0:T(8,128)(2,1)}, bf16[288,576]{1,0:T(8,128)(2,1)}, bf16[288,288]{1,0:T(8,128)(2,1)}, bf16[...) custom-call(s32[16]{0:T(128)} %clip_ref.7, f32[6,96,640]{2,1,0:T(8,128)} %shard_map.101.part_ref, ...), custom_call_target="tpu_custom_call" | custom-call | flops 509607936 | bytes 7048000 | tf_op jit(solution)/shard_map/pallas_call | solution.py:238
  40.8 3.3 %collective-permute-start.2 = (bf16[4,96,256]{2,1,0:T(8,128)(2,1)}, bf16[4,96,256]{2,1,0:T(8,128)(2,1)S(1)}, u32[]{:S(2)}, u32[]{:S(2)}) collective-permute-start(bf16[4,96,256]{2,1,0:T(8,128)(2,1)} %get-tuple-element.26), channel_id=1, source_target_pairs={{1,0},{2,1},{3,2},{4,3},{5,4},{6,5},{7,6},{9,8},{10,9},{11,10},{12... | collective-permute-start | bytes 589832 | tf_op jit(solution)/shard_map/ppermute | solution.py:249
  44.1 5.4 %shard_map.104 = f32[4,96,512]{2,1,0:T(8,128)} custom-call(s32[16]{0:T(128)} %clip_ref.7, bf16[1728,640]{1,0:T(8,128)(2,1)} %get-tuple-element.21.xs_ref, bf16[288,864]{1,0:T(8,128)(2,1)} %get-tuple-element.22.w0_ref, bf16[288,576]{1,0:T(8,128)(2,1)} %get-tuple-element.23.w1_ref, bf16[288,288]{1,0:T(8,128)(2,1)} %get-tuple-element.24.w2_ref, ...), custom_call_target="tpu_custom_call" | custom-call | flops 509607936 | bytes 5210944 | tf_op jit(solution)/shard_map/pallas_call | solution.py:238
  49.5 1.0 %slice.15 = bf16[4,96,256]{2,1,0:T(8,128)(2,1)S(1)} slice(f32[4,96,512]{2,1,0:T(8,128)} %shard_map.104), slice={[0:4], [0:96], [0:256]} | slice | bytes 393216 | tf_op jit(solution)/shard_map/slice | solution.py:311
  50.5 0.1 concatenate.9
  50.6 0.0 collective-permute-done.2
  50.6 1.0 %fusion = bf16[4,96,256]{2,1,0:T(8,128)(2,1)S(1)} fusion(f32[4,96,512]{2,1,0:T(8,128)} %shard_map.104, bf16[4,96,256]{2,1,0:T(8,128)(2,1)S(1)} %collective-permute-done.2), kind=kLoop, calls=%fused_computation.1 | loop fusion | flops 294912 | bytes 786432 | tf_op jit(solution)/shard_map/convert.2
  51.7 0.1 concatenate.10
  51.7 1.2 %pad_maximum_fusion = bf16[4,96,4,128]{3,2,1,0:T(4,128)(2,1)} fusion(bf16[4,96,2,128]{3,2,1,0:T(2,128)(2,1)S(1)} %concatenate.10, bf16[4,96,2,128]{3,2,1,0:T(2,128)(2,1)S(1)} %concatenate.9), kind=kLoop, calls=%fused_computation.3 | loop fusion | flops 786432 | bytes 786432 | tf_op jit(solution)/shard_map/concatenate | solution.py:311
Async XLA Ops:
  9.4 10.8 %collective-permute-start = (bf16[6,96,256]{2,1,0:T(8,128)(2,1)}, bf16[6,96,256]{2,1,0:T(8,128)(2,1)S(1)}, u32[]{:S(2)}, u32[]{:S(2)}) collective-permute-start(bf16[6,96,256]{2,1,0:T(8,128)(2,1)} %get-tuple-element.20), channel_id=1, source_target_pairs={{0,1},{1,2},{2,3},{3,4},{4,5},{5,6},{6,7},{8,9},{9,10},{10,11},{11... | collective-permute-start | bytes 884744 | tf_op jit(solution)/shard_map/ppermute | solution.py:249
  20.3 0.7 %copy-start = (bf16[6,96,256]{2,1,0:T(8,128)(2,1)}, bf16[6,96,256]{2,1,0:T(8,128)(2,1)S(1)}, u32[]{:S(2)}) copy-start(bf16[6,96,256]{2,1,0:T(8,128)(2,1)S(1)} %collective-permute-done.got_ref) | copy-start | bytes 884740
  23.6 10.3 %collective-permute-start.1 = (bf16[4,96,640]{2,1,0:T(8,128)(2,1)}, bf16[4,96,640]{2,1,0:T(8,128)(2,1)S(1)}, u32[]{:S(2)}, u32[]{:S(2)}) collective-permute-start(bf16[4,96,640]{2,1,0:T(8,128)(2,1)} %shard_map.102.mine_ref), channel_id=1, source_target_pairs={{0,8},{8,16},{16,24},{1,9},{9,17},{17,25},{2,10},{10,18},{18,26},{... | collective-permute-start | bytes 1474568 | tf_op jit(solution)/shard_map/ppermute | solution.py:249
  33.9 0.8 %copy-start.1 = (bf16[4,96,640]{2,1,0:T(8,128)(2,1)}, bf16[4,96,640]{2,1,0:T(8,128)(2,1)S(1)}, u32[]{:S(2)}) copy-start(bf16[4,96,640]{2,1,0:T(8,128)(2,1)S(1)} %collective-permute-done.1.before_ref) | copy-start | bytes 1474564
  40.8 9.8 %collective-permute-start.2 = (bf16[4,96,256]{2,1,0:T(8,128)(2,1)}, bf16[4,96,256]{2,1,0:T(8,128)(2,1)S(1)}, u32[]{:S(2)}, u32[]{:S(2)}) collective-permute-start(bf16[4,96,256]{2,1,0:T(8,128)(2,1)} %get-tuple-element.26), channel_id=1, source_target_pairs={{1,0},{2,1},{3,2},{4,3},{5,4},{6,5},{7,6},{9,8},{10,9},{11,10},{12... | collective-permute-start | bytes 589832 | tf_op jit(solution)/shard_map/ppermute | solution.py:249

commit v2 on v1

--- a/solution.py
+++ b/solution.py
@@ -241,6 +241,7 @@
         in_specs=[SMEM] * smem + [VMEM] * (len(operands) - smem),
         out_specs=VMEM if single else tuple(VMEM for _ in shapes),
         cost_estimate=pl.CostEstimate(flops=flops, bytes_accessed=moved, transcendentals=0),
+        compiler_params=pltpu.CompilerParams(vmem_limit_bytes=20 << 20),
     )(*operands)
 
 

time: 53.2 us -> 42.2 us (0.79)
  Pallas kernels: 26.9 us -> 11.2 us
  waiting for transfers between devices: 10.1 us -> 16.1 us
  other arithmetic: 2.2 us -> 1.22 us
    pallas_call x5, Pallas kernels: 26.9 us -> 11.2 us  [call(): pl.pallas_call(kernel, out_shape=shapes[0] if single else tuple(shapes),...]
    ppermute x3, waiting for transfers between devices: 10.1 us -> 16.1 us  [moved_by(): lax.ppermute(block, axis, [(i, i + distance) for i in devices if i + dist...]
    unnamed x4 -> x18, local copies, waits for them, and re-layouts: 1.51 us -> 2.69 us
    slice x1, local copies, waits for them, and re-layouts: 1.02 us -> 0.03 us  [shards(): result = jnp.concatenate([total[:, :, :(height - 2) * width], tail], axis=2)]
    another operation x1, other arithmetic: 1.04 us -> 0.07 us
    reshape x1, local copies, waits for them, and re-layouts: 2.34 us -> 1.65 us  [shards(): lat = latent.reshape(frames, chans, height * width)]
  transfers between devices with their start and end apart: 3 -> 3, of which waited for: 2 -> 3; matrix products, arithmetic and copies ran while one was open for 2% -> 0% of each run, Pallas kernels for 21% -> 12%
where the time goes in v2:
time: 42.2 us; the launch traced here: 41.9 us
  waiting for transfers between devices  16.1 us (38%)
  Pallas kernels  11.2 us (27%)
  starting transfers between devices  8.79 us (21%)
  local copies, waits for them, and re-layouts  4.47 us (11%)
  other arithmetic  1.22 us (3%)
    ppermute x3, waiting for transfers between devices, moved_by(): lax.ppermute(block, axis, [(i, i + distance) for i in devices if i + dist...  16.1 us
    pallas_call x5, Pallas kernels, call(): pl.pallas_call(kernel, out_shape=shapes[0] if single else tuple(shapes),...  11.2 us
    ppermute x3, starting transfers between devices, moved_by(): lax.ppermute(block, axis, [(i, i + distance) for i in devices if i + dist...  8.79 us
    unnamed x18, local copies, waits for them, and re-layouts  2.69 us
    reshape x1, local copies, waits for them, and re-layouts, shards(): lat = latent.reshape(frames, chans, height * width)  1.65 us
    concatenate x1, other arithmetic, shards(): result = jnp.concatenate([total[:, :, :(height - 2) * width], tail], axis=2)  1.16 us
  transfers between devices with their start and end apart: 3, of which 3 were waited for; matrix products, arithmetic and copies ran while one was open for 0% of the time, Pallas kernels for 12%

profile of v2, /device:TPU:22, one launch (start us, length us, event | category | flops | bytes accessed | tf_op | source)
XLA Modules:
  0.0 41.9 jit_solution(9583242474868357816)
XLA Ops:
  0.0 1.6 %reshape.25.lat_ref = bf16[4,192,512]{2,1,0:T(8,128)(2,1)S(1)} reshape(bf16[4,192,4,128]{3,2,1,0:T(4,128)(2,1)} %param.10) | data formatting | bytes 1572864 | tf_op jit(solution)/shard_map/reshape | solution.py:257
  1.7 0.0 copy-start.2
  1.7 0.6 %copy-done.2 = s32[16]{0:T(128)S(1)} copy-done((s32[16]{0:T(128)S(1)}, s32[16]{0:T(128)}, u32[]{:S(2)}) %copy-start.2) | copy-done | bytes 88
  2.3 0.0 copy-start.7
  2.3 1.3 %copy-done.7 = bf16[3,3,3,96,192]{4,3,2,1,0:T(8,128)(2,1)S(1)} copy-done((bf16[3,3,3,96,192]{4,3,2,1,0:T(8,128)(2,1)S(1)}, bf16[3,3,3,96,192]{4,3,2,1,0:T(8,128)(2,1)}, u32[]{:S(2)}) %copy-start.7) | copy-done | bytes 995352
  3.6 0.0 copy-start.8
  3.6 0.7 %copy-done.8 = f32[192]{0:T(256)S(1)} copy-done((f32[192]{0:T(256)S(1)}, f32[192]{0:T(256)}, u32[]{:S(2)}) %copy-start.8) | copy-done | bytes 792
  4.3 3.2 %shard_map.100 = (bf16[2304,512]{1,0:T(8,128)(2,1)S(1)}, bf16[288,1728]{1,0:T(8,128)(2,1)S(1)}, bf16[288,1152]{1,0:T(8,128)(2,1)S(1)}, bf16[6,96,256]{2,1,0:T(8,128)(2,1)S(1)}, f32[6,96,384]{2,1,0:T(8,128)S(1)}) custom-call(s32[16]{0:T(128)S(1)} %copy-done.2, bf16[4,192,512]{2,1,0:T(8,128)(2,1)S(1)} %reshape.25.lat_ref, ...), custom_call_target="tpu_custom_call" | custom-call | flops 1019215872 | bytes 6980416 | tf_op jit(solution)/shard_map/pallas_call | solution.py:238
  7.5 3.4 %collective-permute-start = (bf16[6,96,256]{2,1,0:T(8,128)(2,1)S(1)}, bf16[6,96,256]{2,1,0:T(8,128)(2,1)S(1)}, u32[]{:S(2)}, u32[]{:S(2)}) collective-permute-start(bf16[6,96,256]{2,1,0:T(8,128)(2,1)S(1)} %get-tuple-element.20), channel_id=1, source_target_pairs={{0,1},{1,2},{2,3},{3,4},{4,5},{5,6},{6,7},{8,9},{9,10},{10,11},{11... | collective-permute-start | bytes 884744 | tf_op jit(solution)/shard_map/ppermute | solution.py:250
  10.9 0.0 copy-start.3
  11.0 0.0 copy-start.4
  11.0 2.1 %shard_map.101.part_ref = f32[6,96,640]{2,1,0:T(8,128)S(1)} custom-call(s32[16]{0:T(128)S(1)} %copy-done.2, bf16[2304,512]{1,0:T(8,128)(2,1)S(1)} %get-tuple-element.16.xs_ref, bf16[288,1728]{1,0:T(8,128)(2,1)S(1)} %get-tuple-element.17.wt_ref, bf16[288,1152]{1,0:T(8,128)(2,1)S(1)} %get-tuple-element.18.wu_ref, f32[6,96,384]{2,1,0:T(8,128)S(1)} %get-tuple-element.19.edge_ref), custom_call_target="tpu_custom_call" | custom-call | flops 1019215872 | bytes 6377536 | tf_op jit(solution)/shard_map/pallas_call | solution.py:238
  13.1 0.0 copy-start
  13.1 5.6 %collective-permute-done.got_ref = bf16[6,96,256]{2,1,0:T(8,128)(2,1)S(1)} collective-permute-done((bf16[6,96,256]{2,1,0:T(8,128)(2,1)S(1)}, bf16[6,96,256]{2,1,0:T(8,128)(2,1)S(1)}, u32[]{:S(2)}, u32[]{:S(2)}) %collective-permute-start) | collective-permute-done | bytes 294944 | tf_op jit(solution)/shard_map/ppermute | solution.py:250
  18.7 0.0 copy-done.3
  18.7 0.0 copy-done.4
  18.8 0.3 shard_map.102.mine_ref
  19.1 0.0 copy-start.1
  19.1 0.0 copy-start.5
  19.1 0.0 copy-start.6
  19.1 2.1 %collective-permute-start.1 = (bf16[4,96,640]{2,1,0:T(8,128)(2,1)S(1)}, bf16[4,96,640]{2,1,0:T(8,128)(2,1)S(1)}, u32[]{:S(2)}, u32[]{:S(2)}) collective-permute-start(bf16[4,96,640]{2,1,0:T(8,128)(2,1)S(1)} %shard_map.102.mine_ref), channel_id=1, source_target_pairs={{0,8},{8,16},{16,24},{1,9},{9,17},{17,25},{2,10},{10,18},{18,26},{... | collective-permute-start | bytes 1474568 | tf_op jit(solution)/shard_map/ppermute | solution.py:250
  21.2 8.2 %collective-permute-done.1.before_ref = bf16[4,96,640]{2,1,0:T(8,128)(2,1)S(1)} collective-permute-done((bf16[4,96,640]{2,1,0:T(8,128)(2,1)S(1)}, bf16[4,96,640]{2,1,0:T(8,128)(2,1)S(1)}, u32[]{:S(2)}, u32[]{:S(2)}) %collective-permute-start.1) | collective-permute-done | bytes 491552 | tf_op jit(solution)/shard_map/ppermute | solution.py:250
  29.4 0.0 copy-done
  29.4 2.7 %shard_map.103 = (bf16[1728,640]{1,0:T(8,128)(2,1)S(1)}, bf16[288,864]{1,0:T(8,128)(2,1)S(1)}, bf16[288,576]{1,0:T(8,128)(2,1)S(1)}, bf16[288,288]{1,0:T(8,128)(...) custom-call(s32[16]{0:T(128)S(1)} %copy-done.2, f32[6,96,640]{2,1,0:T(8,128)S(1)} %shard_map.101.part_ref, ...), custom_call_target="tpu_custom_call" | custom-call | flops 509607936 | bytes 7048000 | tf_op jit(solution)/shard_map/pallas_call | solution.py:238
  32.2 3.3 %collective-permute-start.2 = (bf16[4,96,256]{2,1,0:T(8,128)(2,1)S(1)}, bf16[4,96,256]{2,1,0:T(8,128)(2,1)S(1)}, u32[]{:S(2)}, u32[]{:S(2)}) collective-permute-start(bf16[4,96,256]{2,1,0:T(8,128)(2,1)S(1)} %get-tuple-element.26), channel_id=1, source_target_pairs={{1,0},{2,1},{3,2},{4,3},{5,4},{6,5},{7,6},{9,8},{10,9},{11,10},{12... | collective-permute-start | bytes 589832 | tf_op jit(solution)/shard_map/ppermute | solution.py:250
  35.5 0.0 copy-done.1
  35.5 0.0 copy-done.5
  35.5 0.0 copy-done.6
  35.5 2.8 %shard_map.104 = f32[4,96,512]{2,1,0:T(8,128)S(1)} custom-call(s32[16]{0:T(128)S(1)} %copy-done.2, bf16[1728,640]{1,0:T(8,128)(2,1)S(1)} %get-tuple-element.21.xs_ref, bf16[288,864]{1,0:T(8,128)(2,1)S(1)} %get-tuple-element.22.w0_ref, bf16[288,576]{1,0:T(8,128)(2,1)S(1)} %get-tuple-element.23.w1_ref, bf16[288,288]{1,0:T(8,128)(2,1)S(1)} %get-tuple-element.24.w2_ref, ...), custom_call_target="tpu_custom_call" | custom-call | flops 509607936 | bytes 5210944 | tf_op jit(solution)/shard_map/pallas_call | solution.py:238
  38.4 0.1 concatenate.9
  38.4 2.2 %collective-permute-done.2 = bf16[4,96,256]{2,1,0:T(8,128)(2,1)S(1)} collective-permute-done((bf16[4,96,256]{2,1,0:T(8,128)(2,1)S(1)}, bf16[4,96,256]{2,1,0:T(8,128)(2,1)S(1)}, u32[]{:S(2)}, u32[]{:S(2)}) %collective-permute-start.2) | collective-permute-done | bytes 196640 | tf_op jit(solution)/shard_map/ppermute | solution.py:250
  40.6 0.1 fusion
  40.7 0.1 concatenate.10
  40.8 1.2 %pad_maximum_fusion = bf16[4,96,4,128]{3,2,1,0:T(4,128)(2,1)} fusion(bf16[4,96,2,128]{3,2,1,0:T(2,128)(2,1)S(1)} %concatenate.10, bf16[4,96,2,128]{3,2,1,0:T(2,128)(2,1)S(1)} %concatenate.9), kind=kLoop, calls=%fused_computation.3 | loop fusion | flops 786432 | bytes 786432 | tf_op jit(solution)/shard_map/concatenate | solution.py:312
  (1 shorter events, 0.0 us)
Async XLA Ops:
  1.7 0.7 %copy-start.2 = (s32[16]{0:T(128)S(1)}, s32[16]{0:T(128)}, u32[]{:S(2)}) copy-start(s32[16]{0:T(128)} %clip_ref.7) | copy-start | bytes 196
  2.3 1.3 %copy-start.7 = (bf16[3,3,3,96,192]{4,3,2,1,0:T(8,128)(2,1)S(1)}, bf16[3,3,3,96,192]{4,3,2,1,0:T(8,128)(2,1)}, u32[]{:S(2)}) copy-start(bf16[3,3,3,96,192]{4,3,2,1,0:T(8,128)(2,1)} %weight_ref.2) | copy-start | bytes 2985988
  3.6 0.7 %copy-start.8 = (f32[192]{0:T(256)S(1)}, f32[192]{0:T(256)}, u32[]{:S(2)}) copy-start(f32[192]{0:T(256)} %param.12) | copy-start | bytes 2308
  7.5 11.2 %collective-permute-start = (bf16[6,96,256]{2,1,0:T(8,128)(2,1)S(1)}, bf16[6,96,256]{2,1,0:T(8,128)(2,1)S(1)}, u32[]{:S(2)}, u32[]{:S(2)}) collective-permute-start(bf16[6,96,256]{2,1,0:T(8,128)(2,1)S(1)} %get-tuple-element.20), channel_id=1, source_target_pairs={{0,1},{1,2},{2,3},{3,4},{4,5},{5,6},{6,7},{8,9},{9,10},{10,11},{11... | collective-permute-start | bytes 884744 | tf_op jit(solution)/shard_map/ppermute | solution.py:250
  10.9 7.8 %copy-start.3 = (f32[96]{0:T(128)S(1)}, f32[96]{0:T(128)}, u32[]{:S(2)}) copy-start(f32[96]{0:T(128)} %param.14) | copy-start | bytes 1156
  11.0 7.8 %copy-start.4 = (f32[96]{0:T(128)S(1)}, f32[96]{0:T(128)}, u32[]{:S(2)}) copy-start(f32[96]{0:T(128)} %param.15) | copy-start | bytes 1156
  13.1 16.3 %copy-start = (bf16[3,3,3,96,96]{4,3,2,1,0:T(8,128)(2,1)S(1)}, bf16[3,3,3,96,96]{4,3,2,1,0:T(8,128)(2,1)}, u32[]{:S(2)}) copy-start(bf16[3,3,3,96,96]{4,3,2,1,0:T(8,128)(2,1)} %weight_ref.3) | copy-start | bytes 1492996
  19.1 16.4 %copy-start.1 = (bf16[96,192]{1,0:T(8,128)(2,1)S(1)}, bf16[96,192]{1,0:T(8,128)(2,1)}, u32[]{:S(2)}) copy-start(bf16[96,192]{1,0:T(8,128)(2,1)} %skip_ref.1) | copy-start | bytes 110596
  19.1 16.4 %copy-start.5 = (f32[96]{0:T(128)S(1)}, f32[96]{0:T(128)}, u32[]{:S(2)}) copy-start(f32[96]{0:T(128)} %param.17) | copy-start | bytes 1156
  19.1 16.4 %copy-start.6 = (f32[96]{0:T(128)S(1)}, f32[96]{0:T(128)}, u32[]{:S(2)}) copy-start(f32[96]{0:T(128)} %param.19) | copy-start | bytes 1156
  19.1 10.3 %collective-permute-start.1 = (bf16[4,96,640]{2,1,0:T(8,128)(2,1)S(1)}, bf16[4,96,640]{2,1,0:T(8,128)(2,1)S(1)}, u32[]{:S(2)}, u32[]{:S(2)}) collective-permute-start(bf16[4,96,640]{2,1,0:T(8,128)(2,1)S(1)} %shard_map.102.mine_ref), channel_id=1, source_target_pairs={{0,8},{8,16},{16,24},{1,9},{9,17},{17,25},{2,10},{10,18},{18,26},{... | collective-permute-start | bytes 1474568 | tf_op jit(solution)/shard_map/ppermute | solution.py:250
  32.2 8.5 %collective-permute-start.2 = (bf16[4,96,256]{2,1,0:T(8,128)(2,1)S(1)}, bf16[4,96,256]{2,1,0:T(8,128)(2,1)S(1)}, u32[]{:S(2)}, u32[]{:S(2)}) collective-permute-start(bf16[4,96,256]{2,1,0:T(8,128)(2,1)S(1)} %get-tuple-element.26), channel_id=1, source_target_pairs={{1,0},{2,1},{3,2},{4,3},{5,4},{6,5},{7,6},{9,8},{10,9},{11,10},{12... | collective-permute-start | bytes 589832 | tf_op jit(solution)/shard_map/ppermute | solution.py:250

commit v3 on v2

v3 whole, which is shorter than its diff:
```python
import jax
import jax.numpy as jnp
from jax import lax
from jax.experimental import pallas as pl
from jax.experimental.pallas import tpu as pltpu
from jax.sharding import PartitionSpec as P

F32 = jnp.float32
BF16 = jnp.bfloat16
VMEM = pl.BlockSpec(memory_space=pltpu.VMEM)
SMEM = pl.BlockSpec(memory_space=pltpu.SMEM)
HBM = pl.BlockSpec(memory_space=pltpu.HBM)


def silu_norm(values, gain):
    mean_sq = jnp.mean(values * values, axis=0, keepdims=True)
    scaled = values * lax.rsqrt(mean_sq + 1e-06) * gain
    return scaled / (1.0 + jnp.exp(-scaled))


def column_taps(act):
    lane = lax.broadcasted_iota(jnp.int32, act.shape, 1)
    width = act.shape[1]
    left = jnp.where(lane == 0, 0.0, pltpu.roll(act, 1, 1))
    right = jnp.where(lane == width - 1, 0.0, pltpu.roll(act, width - 1, 1))
    return left.astype(BF16), act.astype(BF16), right.astype(BF16)


def spread(vector, width):
    return jnp.broadcast_to(vector, (width, vector.shape[1])).T


def kept(clip_ref, frame, back):
    final = clip_ref.shape[0] - 1
    here = clip_ref[jnp.clip(frame, 0, final)]
    there = clip_ref[jnp.clip(frame - back, 0, final)]
    return (frame - back >= 0) & (here == there)


def fold_taps(weight_ref, row_tap, first, last):
    return jnp.concatenate([weight_ref[t, row_tap, j] for t in range(first, last + 1) for j in range(3)], axis=1)


def dot(a, b):
    return jnp.dot(a, b, preferred_element_type=F32)


def by_suffix(clip_ref, frame, first, last, body, nothing):
    flags = [None if t == 2 else kept(clip_ref, frame, 2 - t) for t in range(first, last + 1)]
    prior = None
    for t, flag in zip(range(first, last + 1), flags):
        here = flag if prior is None else (~prior if flag is None else ~prior & flag)
        if here is None:
            body(t)
            return
        pl.when(here)(lambda t=t: body(t))
        prior = flag
    if last != 2:
        pl.when(~prior)(nothing)


def norm_frame(lat_ref, frame, rows, gain, xs_ref):
    _, chans, height, width = lat_ref.shape
    values = lat_ref[frame].reshape(chans, height * width)
    for n, r in enumerate(rows):
        act = silu_norm(values[:, r * width : (r + 1) * width].astype(F32), gain)
        for j, tap in enumerate(column_taps(act)):
            xs_ref[pl.ds((frame * 3 + j) * chans, chans), n * width : (n + 1) * width] = tap


def conv_first(xs_ref, wt_ref, wu_ref, clip_ref, start, frames, emit):
    depth = xs_ref.shape[0] // frames
    for out in range(frames + 2):
        first, last = max(0, 2 - out), min(2, frames + 1 - out)

        def body(t, out=out, last=last):
            rows = pl.ds((out - 2 + t) * depth, (last + 1 - t) * depth)
            if t == 1:
                weight = wu_ref[:, : (last + 1 - t) * depth]
            else:
                weight = wt_ref[:, t * depth : (last + 1) * depth]
            emit(out, dot(weight, xs_ref[rows, :]))

        def nothing(out=out):
            emit(out, jnp.zeros((wt_ref.shape[0], xs_ref.shape[1]), F32))

        by_suffix(clip_ref, start + out, first, last, body, nothing)


def first_kernel(clip_hbm, lat_hbm, weight_hbm, gain_hbm, wt_ref, wu_ref, up_ref, edge_ref, lat_ref, xs_ref, weight_ref, gain_ref, clip_ref, sems):
    frames, chans, height, width = lat_ref.shape
    outs = weight_ref.shape[3]
    start = lax.axis_index("tm") * frames
    pairs = [(gain_hbm, gain_ref)] + [(lat_hbm.at[f], lat_ref.at[f]) for f in range(frames)]
    pairs += [(clip_hbm, clip_ref), (weight_hbm, weight_ref)]
    copies = [pltpu.make_async_copy(a, b, sems.at[n]) for n, (a, b) in enumerate(pairs)]
    for copy in copies:
        copy.start()
    copies[0].wait()
    gain = spread(gain_ref[...], width)
    for f in range(frames):
        copies[1 + f].wait()
        norm_frame(lat_ref, f, (height - 2, height - 1), gain, xs_ref)
    for copy in copies[1 + frames :]:
        copy.wait()
    for i in range(3):
        wt_ref[i * outs : (i + 1) * outs, :] = fold_taps(weight_ref, i, 0, 2)
        wu_ref[i * outs : (i + 1) * outs, :] = fold_taps(weight_ref, i, 1, 2)

    def emit(out, y):
        y0, y1, y2 = (y[i * outs : (i + 1) * outs] for i in range(3))
        far = y0[:, :width] + y1[:, width:]
        up_ref[out, :, :width] = far.astype(BF16)
        up_ref[out, :, width:] = y0[:, width:].astype(BF16)
        edge_ref[out, :, :width] = y2[:, :width]
        edge_ref[out, :, width : 2 * width] = y1[:, :width] + y2[:, width:]
        edge_ref[out, :, 2 * width :] = far

    conv_first(xs_ref, wt_ref, wu_ref, clip_ref, start, frames, emit)


def inner_kernel(clip_ref, lat_ref, gain_ref, wt_ref, wu_ref, edge_ref, bias_ref, gain_mid_ref, part_ref, early_ref, xs_ref):
    frames, chans, height, width = lat_ref.shape
    outs = edge_ref.shape[1]
    inner = height - 2
    start = lax.axis_index("tm") * frames
    gain = spread(gain_ref[...], width)
    bias, gain_mid = spread(bias_ref[...], width), spread(gain_mid_ref[...], width)
    for f in range(frames):
        norm_frame(lat_ref, f, range(inner), gain, xs_ref)

    def emit(out, y):
        y0, y1, y2 = (y[i * outs : (i + 1) * outs] for i in range(3))
        for h in range(-1, inner + 2):
            total = None
            for tap, row in ((y0, h - 1), (y1, h), (y2, h + 1)):
                if 0 <= row < inner:
                    term = tap[:, row * width : (row + 1) * width]
                    total = term if total is None else total + term
            if h >= inner - 1:
                e = h - inner + 1
                term = edge_ref[out, :, e * width : (e + 1) * width]
                total = term if total is None else total + term
            part_ref[out, :, (h + 1) * width : (h + 2) * width] = total

    conv_first(xs_ref, wt_ref, wu_ref, clip_ref, start, frames, emit)
    for k in range(4):
        for h in range(1, height):
            total = part_ref[frames - 2 + k, :, (h + 1) * width : (h + 2) * width]
            if k < 2:
                total = act_rows(total, h, height, bias, gain_mid)
            early_ref[k, :, (h - 1) * width : h * width] = total.astype(BF16)


def act_rows(total, h, height, bias, gain):
    hidden = (total + bias).astype(BF16).astype(F32)
    act = silu_norm(hidden, gain)
    if h == -1:
        return jnp.where(lax.axis_index("rows") > 0, act, 0.0)
    if h == height - 1:
        return jnp.where(lax.axis_index("rows") == lax.axis_size("rows") - 1, act, 0.0)
    return act


def hidden_sum(part_ref, got_ref, out, h, width):
    total = part_ref[out, :, (h + 1) * width : (h + 2) * width]
    if h < 1:
        total = total + got_ref[out, :, (h + 1) * width : (h + 2) * width].astype(F32)
    return total


def late_kernel(part_ref, got_ref, bias_ref, gain_ref, late_ref):
    width = got_ref.shape[2] // 2
    frames = part_ref.shape[0] - 2
    height = part_ref.shape[2] // width - 1
    bias, gain = spread(bias_ref[...], width), spread(gain_ref[...], width)
    for k in range(4):
        for h in (-1, 0):
            total = hidden_sum(part_ref, got_ref, frames - 2 + k, h, width)
            if k < 2:
                total = act_rows(total, h, height, bias, gain)
            late_ref[k, :, (h + 1) * width : (h + 2) * width] = total.astype(BF16)


def conv_second(xs_ref, wt_refs, clip_ref, start, frames, emit):
    depth = xs_ref.shape[0] // (frames + 2)
    for out in range(frames):

        def body(t, out=out):
            rows = pl.ds((out + t) * depth, (3 - t) * depth)
            emit(out, dot(wt_refs[t][...], xs_ref[rows, :]))

        by_suffix(clip_ref, start + out, 0, 2, body, None)


def act_taps(mine_ref, before_ref, sums, rows, height, bias, gain, frames, xs_ref):
    outs = mine_ref.shape[1]
    width = mine_ref.shape[2] // len(rows)
    for s in range(-2, frames):
        for n, h in enumerate(rows):
            cols = pl.ds(n * width, width)
            if s < 0:
                act = before_ref[s + 2, :, cols].astype(F32)
            elif s >= frames - 2:
                act = mine_ref[s - frames + 2, :, cols].astype(F32)
            else:
                total = sums(s, h)
                if s < 2:
                    total = total + before_ref[2 + s, :, cols].astype(F32)
                act = act_rows(total, h, height, bias, gain)
            for j, tap in enumerate(column_taps(act)):
                xs_ref[pl.ds(((s + 2) * 3 + j) * outs, outs), cols] = tap


def body_kernel(clip_ref, part_ref, mine_ref, before_ref, weight_ref, bias_ref, gain_ref, lat_ref, skip_ref, bias_mid_ref, skip_bias_ref, w0_ref, w1_ref, w2_ref, total_ref, xs_ref):
    frames, chans, height, width = lat_ref.shape
    outs = part_ref.shape[1]
    start = lax.axis_index("tm") * frames
    bias, gain = spread(bias_ref[...], width), spread(gain_ref[...], width)
    shift = spread(bias_mid_ref[...] + skip_bias_ref[...], width)
    refs = (w0_ref, w1_ref, w2_ref)
    for t, ref in enumerate(refs):
        for i in range(3):
            ref[i * outs : (i + 1) * outs, :] = fold_taps(weight_ref, i, t, 2)
    sums = lambda s, h: part_ref[s, :, (h + 1) * width : (h + 2) * width]
    act_taps(mine_ref, before_ref, sums, range(1, height), height, bias, gain, frames, xs_ref)
    skip = skip_ref[...]

    def emit(out, y):
        y0, y1, y2 = (y[i * outs : (i + 1) * outs] for i in range(3))
        short = dot(skip, lat_ref[out].reshape(chans, height * width))
        for r in range(height):
            total = short[:, r * width : (r + 1) * width] + shift
            for tap, row in ((y0, r - 1), (y1, r), (y2, r + 1)):
                if 1 <= row < height:
                    total = total + tap[:, (row - 1) * width : row * width]
            total_ref[out, :, r * width : (r + 1) * width] = total

    conv_second(xs_ref, refs, clip_ref, start, frames, emit)


def edge_kernel(clip_ref, part_ref, got_ref, mine_ref, before_ref, bias_ref, gain_ref, w0_ref, w1_ref, w2_ref, down_ref, edge_ref, xs_ref):
    width = got_ref.shape[2] // 2
    frames = part_ref.shape[0] - 2
    height = part_ref.shape[2] // width - 1
    outs = part_ref.shape[1]
    start = lax.axis_index("tm") * frames
    bias, gain = spread(bias_ref[...], width), spread(gain_ref[...], width)
    sums = lambda s, h: hidden_sum(part_ref, got_ref, s, h, width)
    act_taps(mine_ref, before_ref, sums, (-1, 0), height, bias, gain, frames, xs_ref)

    def emit(out, y):
        y0, y1, y2 = (y[i * outs : (i + 1) * outs] for i in range(3))
        down_ref[out, :, :width] = y2[:, :width].astype(BF16)
        down_ref[out, :, width:] = (y1[:, :width] + y2[:, width:]).astype(BF16)
        edge_ref[out, :, :width] = y0[:, :width] + y1[:, width:]
        edge_ref[out, :, width:] = y0[:, width:]

    conv_second(xs_ref, (w0_ref, w1_ref, w2_ref), clip_ref, start, frames, emit)


def last_kernel(total_ref, edge_ref, below_ref, out_ref):
    frames, outs, height, width = out_ref.shape
    for f in range(frames):
        rows = [total_ref[f, :, r * width : (r + 1) * width] for r in range(height)]
        for n in range(2):
            cols = pl.ds(n * width, width)
            rows[n] = rows[n] + edge_ref[f, :, cols]
            rows[height - 2 + n] = rows[height - 2 + n] + below_ref[f, :, cols].astype(F32)
        out_ref[f] = jnp.concatenate(rows, axis=1).reshape(outs, height, width).astype(BF16)


def call(kernel, shapes, operands, flops, places=(), scratch=()):
    moved = sum(x.size * x.dtype.itemsize for x in operands) + sum(s.size * s.dtype.itemsize for s in shapes)
    single = len(shapes) == 1
    places = list(places) + [VMEM] * (len(operands) - len(places))
    return pl.pallas_call(
        kernel,
        out_shape=shapes[0] if single else tuple(shapes),
        in_specs=places,
        out_specs=VMEM if single else tuple(VMEM for _ in shapes),
        scratch_shapes=list(scratch),
        cost_estimate=pl.CostEstimate(flops=flops, bytes_accessed=moved, transcendentals=0),
        compiler_params=pltpu.CompilerParams(vmem_limit_bytes=20 << 20),
    )(*operands)


def moved_by(block, axis, distance):
    devices = range(lax.axis_size(axis))
    return lax.ppermute(block, axis, [(i, i + distance) for i in devices if i + distance in devices])


def shards(latent, clip_ids, gain_in, conv_in, bias_in, gain_mid, conv_mid, bias_mid, skip_weight, skip_bias):
    frames, chans, height, width = latent.shape
    outs = conv_in.shape[3]
    shape = jax.ShapeDtypeStruct
    row = lambda v: v.reshape(1, -1)
    deep, deep_mid, tall = 3 * chans, 3 * outs, 3 * outs
    work = 2 * tall * 3 * deep * frames * width
    wt, wu, up, edge, lat = call(
        first_kernel,
        [
            shape((tall, 3 * deep), BF16),
            shape((tall, 2 * deep), BF16),
            shape((frames + 2, outs, 2 * width), BF16),
            shape((frames + 2, outs, 3 * width), F32),
            shape(latent.shape, BF16),
        ],
        tuple(pltpu.with_memory_space_constraint(x, pltpu.HBM) for x in (clip_ids, latent, conv_in, row(gain_in))),
        work * 2,
        [HBM] * 4,
        [
            pltpu.VMEM((frames * deep, 2 * width), BF16),
            pltpu.VMEM(conv_in.shape, BF16),
            pltpu.VMEM((1, chans), F32),
            pltpu.SMEM(clip_ids.shape, jnp.int32),
            pltpu.SemaphoreType.DMA((frames + 3,)),
        ],
    )
    got = moved_by(up, "rows", 1)
    part, early = call(
        inner_kernel,
        [shape((frames + 2, outs, (height + 1) * width), F32), shape((4, outs, (height - 1) * width), BF16)],
        (clip_ids, lat, row(gain_in), wt, wu, edge, row(bias_in), row(gain_mid)),
        work * (height - 2),
        [SMEM],
        [pltpu.VMEM((frames * deep, (height - 2) * width), BF16)],
    )
    before_early = moved_by(early, "tm", 1)
    late = call(
        late_kernel,
        [shape((4, outs, 2 * width), BF16)],
        (part, got, row(bias_in), row(gain_mid)),
        1000,
    )
    before_late = moved_by(late, "tm", 1)
    w0, w1, w2, total = call(
        body_kernel,
        [
            shape((tall, 3 * deep_mid), BF16),
            shape((tall, 2 * deep_mid), BF16),
            shape((tall, deep_mid), BF16),
            shape((frames, outs, height * width), F32),
        ],
        (clip_ids, part, early, before_early, conv_mid, row(bias_in), row(gain_mid), lat, skip_weight, row(bias_mid), row(skip_bias)),
        work * (height - 1) // 2,
        [SMEM],
        [pltpu.VMEM(((frames + 2) * deep_mid, (height - 1) * width), BF16)],
    )
    down, edge_mid = call(
        edge_kernel,
        [shape((frames, outs, 2 * width), BF16), shape((frames, outs, 2 * width), F32)],
        (clip_ids, part, got, late, before_late, row(bias_in), row(gain_mid), w0, w1, w2),
        work,
        [SMEM],
        [pltpu.VMEM(((frames + 2) * deep_mid, 2 * width), BF16)],
    )
    below = moved_by(down, "rows", -1)
    return call(last_kernel, [shape((frames, outs, height, width), BF16)], (total, edge_mid, below), 1000)


def solution(mesh):
    return jax.shard_map(
        shards,
        mesh=mesh,
        in_specs=(P("tm", None, "rows", None), P(), P(), P(), P(), P(), P(), P(), P(), P()),
        out_specs=P("tm", None, "rows", None),
        check_vma=False,
    )
```

time: 42.2 us -> 34.9 us (0.83)
  waiting for transfers between devices: 16.1 us -> 9.71 us
  local copies, waits for them, and re-layouts: 4.47 us -> 0.04 us
  Pallas kernels: 11.2 us -> 14.5 us
  starting transfers between devices: 8.79 us -> 10.1 us
  other arithmetic: 1.22 us -> 0 us
    ppermute x3 -> x4, waiting for transfers between devices: 16.1 us -> 9.71 us  [moved_by(): lax.ppermute(block, axis, [(i, i + distance) for i in devices if i + dist...]
    pallas_call x5 -> x6, Pallas kernels: 11.2 us -> 14.5 us  [call(): pl.pallas_call(kernel, out_shape=shapes[0] if single else tuple(shapes),...]
    unnamed x18 -> x16, local copies, waits for them, and re-layouts: 2.69 us -> 0.04 us
    reshape x1 -> x0, local copies, waits for them, and re-layouts: 1.65 us -> none  [shards(): lat = latent.reshape(frames, chans, height * width)]
    ppermute x3 -> x4, starting transfers between devices: 8.79 us -> 10.1 us  [moved_by(): lax.ppermute(block, axis, [(i, i + distance) for i in devices if i + dist...]
    concatenate x1 -> x0, other arithmetic: 1.16 us -> none  [shards(): result = jnp.concatenate([total[:, :, :(height - 2) * width], tail], axis=2)]
  transfers between devices with their start and end apart: 3 -> 4, of which waited for: 3 -> 3; matrix products, arithmetic and copies ran while one was open for 0% -> 0% of each run, Pallas kernels for 12% -> 20%
where the time goes in v3:
time: 34.9 us; the launch traced here: 34.5 us
  Pallas kernels  14.5 us (42%)
  starting transfers between devices  10.1 us (29%)
  waiting for transfers between devices  9.71 us (28%)
    pallas_call x6, Pallas kernels, call(): pl.pallas_call(kernel, out_shape=shapes[0] if single else tuple(shapes),...  14.5 us
    ppermute x4, starting transfers between devices, moved_by(): lax.ppermute(block, axis, [(i, i + distance) for i in devices if i + dist...  10.1 us
    ppermute x4, waiting for transfers between devices, moved_by(): lax.ppermute(block, axis, [(i, i + distance) for i in devices if i + dist...  9.71 us
  transfers between devices with their start and end apart: 4, of which 3 were waited for; matrix products, arithmetic and copies ran while one was open for 0% of the time, Pallas kernels for 20%

profile of v3, /device:TPU:22, one launch (start us, length us, event | category | flops | bytes accessed | tf_op | source)
XLA Modules:
  0.0 34.5 jit_solution(11866202130588864491)
XLA Ops:
  0.0 0.0 copy-start.2
  0.0 0.0 copy-start.3
  0.0 0.0 copy-start.4
  0.0 0.0 copy-start.7
  0.0 4.5 %shard_map.100 = (bf16[288,1728]{1,0:T(8,128)(2,1)S(1)}, bf16[288,1152]{1,0:T(8,128)(2,1)S(1)}, bf16[6,96,256]{2,1,0:T(8,128)(2,1)S(1)}, f32[6,96,384]{2,1,0:T(8,128)S(1)}, bf16[4,192,4,128]{3,2,1,0:T(4,128)(2,1)S(1)}) custom-call(s32[16]{0:T(128)} %clip_ref.5, bf16[4,192,4,128]{3,2,1,0:T(4,128)(2,1)} %lat_hbm.1, bf16[3,3,3,96,192]{4,3,2,1,0:T(8,128)(2,1)} %weight_hbm.1, ...), custom_call_target="tpu_custom_call" | custom-call | flops 1019215872 | bytes 5407552 | tf_op jit(solution)/shard_map/pallas_call | solution.py:277
  4.5 3.4 %collective-permute-start.1 = (bf16[6,96,256]{2,1,0:T(8,128)(2,1)S(1)}, bf16[6,96,256]{2,1,0:T(8,128)(2,1)S(1)}, u32[]{:S(2)}, u32[]{:S(2)}) collective-permute-start(bf16[6,96,256]{2,1,0:T(8,128)(2,1)S(1)} %get-tuple-element.25), channel_id=1, source_target_pairs={{0,1},{1,2},{2,3},{3,4},{4,5},{5,6},{6,7},{8,9},{9,10},{10,11},{11... | collective-permute-start | bytes 884744 | tf_op jit(solution)/shard_map/ppermute | solution.py:290
  8.0 0.0 copy-done.2
  8.0 0.0 copy-done.3
  8.0 0.0 copy-done.4
  8.0 0.0 copy-done.7
  8.0 3.6 %shard_map.101 = (f32[6,96,640]{2,1,0:T(8,128)S(1)}, bf16[4,96,384]{2,1,0:T(8,128)(2,1)S(1)}) custom-call(s32[16]{0:T(128)S(1)} %copy-done.4, bf16[4,192,4,128]{3,2,1,0:T(4,128)(2,1)S(1)} %get-tuple-element.18.lat_ref, f32[1,192]{1,0:T(1,128)S(1)} %bitcast.16, bf16[288,1728]{1,0:T(8,128)(2,1)S(1)} %get-tuple-element.19.wt_ref, ...), custom_call_target="tpu_custom_call" | custom-call | flops 1019215872 | bytes 5101120 | tf_op jit(solution)/shard_map/pallas_call | solution.py:277
  11.6 0.0 copy-start
  11.6 0.0 copy-start.1
  11.6 0.0 copy-start.5
  11.7 0.0 copy-start.6
  11.7 2.1 %collective-permute-start = (bf16[4,96,384]{2,1,0:T(8,128)(2,1)S(1)}, bf16[4,96,384]{2,1,0:T(8,128)(2,1)S(1)}, u32[]{:S(2)}, u32[]{:S(2)}) collective-permute-start(bf16[4,96,384]{2,1,0:T(8,128)(2,1)S(1)} %get-tuple-element.23.mine_ref), channel_id=1, source_target_pairs={{0,8},{8,16},{16,24},{1,9},{9,17},{17,25},{2,10},{10,18},{18,26},{... | collective-permute-start | bytes 884744 | tf_op jit(solution)/shard_map/ppermute | solution.py:290
  13.7 1.5 %collective-permute-done.1.got_ref = bf16[6,96,256]{2,1,0:T(8,128)(2,1)S(1)} collective-permute-done((bf16[6,96,256]{2,1,0:T(8,128)(2,1)S(1)}, bf16[6,96,256]{2,1,0:T(8,128)(2,1)S(1)}, u32[]{:S(2)}, u32[]{:S(2)}) %collective-permute-start.1) | collective-permute-done | bytes 294944 | tf_op jit(solution)/shard_map/ppermute | solution.py:290
  15.2 0.2 shard_map.103.mine_ref
  15.4 1.9 %collective-permute-start.2 = (bf16[4,96,256]{2,1,0:T(8,128)(2,1)S(1)}, bf16[4,96,256]{2,1,0:T(8,128)(2,1)S(1)}, u32[]{:S(2)}, u32[]{:S(2)}) collective-permute-start(bf16[4,96,256]{2,1,0:T(8,128)(2,1)S(1)} %shard_map.103.mine_ref), channel_id=1, source_target_pairs={{0,8},{8,16},{16,24},{1,9},{9,17},{17,25},{2,10},{10,18},{18,26},{... | collective-permute-start | bytes 589832 | tf_op jit(solution)/shard_map/ppermute | solution.py:290
  17.3 2.5 %collective-permute-done.before_ref = bf16[4,96,384]{2,1,0:T(8,128)(2,1)S(1)} collective-permute-done((bf16[4,96,384]{2,1,0:T(8,128)(2,1)S(1)}, bf16[4,96,384]{2,1,0:T(8,128)(2,1)S(1)}, u32[]{:S(2)}, u32[]{:S(2)}) %collective-permute-start) | collective-permute-done | bytes 294944 | tf_op jit(solution)/shard_map/ppermute | solution.py:290
  19.8 0.0 copy-done
  19.8 0.0 copy-done.1
  19.9 0.0 copy-done.5
  19.9 0.0 copy-done.6
  19.9 3.1 %shard_map.102 = (bf16[288,864]{1,0:T(8,128)(2,1)S(1)}, bf16[288,576]{1,0:T(8,128)(2,1)S(1)}, bf16[288,288]{1,0:T(8,128)(2,1)S(1)}, f32[4,96,512]{2,1,0:T(8,128)S(1)}) custom-call(s32[16]{0:T(128)S(1)} %copy-done.4, f32[6,96,640]{2,1,0:T(8,128)S(1)} %get-tuple-element.22.part_ref, bf16[4,96,384]{2,1,0:T(8,128)(2,1)S(1)} %get-tuple-element.23.mine_ref, ...), custom_call_target="tpu_custom_call" | custom-call | flops 764411904 | bytes 5168704 | tf_op jit(solution)/shard_map/pallas_call | solution.py:277
  23.0 0.0 collective-permute-done.2.before_ref
  23.0 2.1 %shard_map.104 = (bf16[4,96,256]{2,1,0:T(8,128)(2,1)S(1)}, f32[4,96,256]{2,1,0:T(8,128)S(1)}) custom-call(s32[16]{0:T(128)S(1)} %copy-done.4, f32[6,96,640]{2,1,0:T(8,128)S(1)} %get-tuple-element.22.part_ref, bf16[6,96,256]{2,1,0:T(8,128)(2,1)S(1)} %collective-permute-done.1.got_ref, bf16[4,96,256]{2,1,0:T(8,128)(2,1)S(1)} %shard_map.103.mine_ref, ...), custom_call_target="tpu_custom_call" | custom-call | flops 509607936 | bytes 3748672 | tf_op jit(solution)/shard_map/pallas_call | solution.py:277
  25.1 2.7 %collective-permute-start.3 = (bf16[4,96,256]{2,1,0:T(8,128)(2,1)S(1)}, bf16[4,96,256]{2,1,0:T(8,128)(2,1)S(1)}, u32[]{:S(2)}, u32[]{:S(2)}) collective-permute-start(bf16[4,96,256]{2,1,0:T(8,128)(2,1)S(1)} %get-tuple-element.30), channel_id=1, source_target_pairs={{1,0},{2,1},{3,2},{4,3},{5,4},{6,5},{7,6},{9,8},{10,9},{11,10},{12... | collective-permute-start | bytes 589832 | tf_op jit(solution)/shard_map/ppermute | solution.py:290
  27.8 5.7 %collective-permute-done.3.below_ref = bf16[4,96,256]{2,1,0:T(8,128)(2,1)S(1)} collective-permute-done((bf16[4,96,256]{2,1,0:T(8,128)(2,1)S(1)}, bf16[4,96,256]{2,1,0:T(8,128)(2,1)S(1)}, u32[]{:S(2)}, u32[]{:S(2)}) %collective-permute-start.3) | collective-permute-done | bytes 196640 | tf_op jit(solution)/shard_map/ppermute | solution.py:290
  33.5 1.0 %shard_map.105 = bf16[4,96,4,128]{3,2,1,0:T(4,128)(2,1)} custom-call(f32[4,96,512]{2,1,0:T(8,128)S(1)} %get-tuple-element.24.total_ref, f32[4,96,256]{2,1,0:T(8,128)S(1)} %get-tuple-element.29.edge_ref, bf16[4,96,256]{2,1,0:T(8,128)(2,1)S(1)} %collective-permute-done.3.below_ref), custom_call_target="tpu_custom_call" | custom-call | flops 1000 | bytes 1769472 | tf_op jit(solution)/shard_map/pallas_call | solution.py:277
Async XLA Ops:
  0.0 8.0 %copy-start.2 = (f32[96]{0:T(128)S(1)}, f32[96]{0:T(128)}, u32[]{:S(2)}) copy-start(f32[96]{0:T(128)} %param.14) | copy-start | bytes 1156
  0.0 8.0 %copy-start.3 = (f32[96]{0:T(128)S(1)}, f32[96]{0:T(128)}, u32[]{:S(2)}) copy-start(f32[96]{0:T(128)} %param.15) | copy-start | bytes 1156
  0.0 8.0 %copy-start.4 = (s32[16]{0:T(128)S(1)}, s32[16]{0:T(128)}, u32[]{:S(2)}) copy-start(s32[16]{0:T(128)} %clip_ref.5) | copy-start | bytes 196
  0.0 8.0 %copy-start.7 = (f32[192]{0:T(256)S(1)}, f32[192]{0:T(256)}, u32[]{:S(2)}) copy-start(f32[192]{0:T(256)} %param.12) | copy-start | bytes 2308
  4.5 10.6 %collective-permute-start.1 = (bf16[6,96,256]{2,1,0:T(8,128)(2,1)S(1)}, bf16[6,96,256]{2,1,0:T(8,128)(2,1)S(1)}, u32[]{:S(2)}, u32[]{:S(2)}) collective-permute-start(bf16[6,96,256]{2,1,0:T(8,128)(2,1)S(1)} %get-tuple-element.25), channel_id=1, source_target_pairs={{0,1},{1,2},{2,3},{3,4},{4,5},{5,6},{6,7},{8,9},{9,10},{10,11},{11... | collective-permute-start | bytes 884744 | tf_op jit(solution)/shard_map/ppermute | solution.py:290
  11.6 8.2 %copy-start = (bf16[3,3,3,96,96]{4,3,2,1,0:T(8,128)(2,1)S(1)}, bf16[3,3,3,96,96]{4,3,2,1,0:T(8,128)(2,1)}, u32[]{:S(2)}) copy-start(bf16[3,3,3,96,96]{4,3,2,1,0:T(8,128)(2,1)} %weight_ref.1) | copy-start | bytes 1492996
  11.6 8.2 %copy-start.1 = (bf16[96,192]{1,0:T(8,128)(2,1)S(1)}, bf16[96,192]{1,0:T(8,128)(2,1)}, u32[]{:S(2)}) copy-start(bf16[96,192]{1,0:T(8,128)(2,1)} %skip_ref.1) | copy-start | bytes 110596
  11.6 8.2 %copy-start.5 = (f32[96]{0:T(128)S(1)}, f32[96]{0:T(128)}, u32[]{:S(2)}) copy-start(f32[96]{0:T(128)} %param.17) | copy-start | bytes 1156
  11.7 8.2 %copy-start.6 = (f32[96]{0:T(128)S(1)}, f32[96]{0:T(128)}, u32[]{:S(2)}) copy-start(f32[96]{0:T(128)} %param.19) | copy-start | bytes 1156
  11.7 8.2 %collective-permute-start = (bf16[4,96,384]{2,1,0:T(8,128)(2,1)S(1)}, bf16[4,96,384]{2,1,0:T(8,128)(2,1)S(1)}, u32[]{:S(2)}, u32[]{:S(2)}) collective-permute-start(bf16[4,96,384]{2,1,0:T(8,128)(2,1)S(1)} %get-tuple-element.23.mine_ref), channel_id=1, source_target_pairs={{0,8},{8,16},{16,24},{1,9},{9,17},{17,25},{2,10},{10,18},{18,26},{... | collective-permute-start | bytes 884744 | tf_op jit(solution)/shard_map/ppermute | solution.py:290
  15.4 7.6 %collective-permute-start.2 = (bf16[4,96,256]{2,1,0:T(8,128)(2,1)S(1)}, bf16[4,96,256]{2,1,0:T(8,128)(2,1)S(1)}, u32[]{:S(2)}, u32[]{:S(2)}) collective-permute-start(bf16[4,96,256]{2,1,0:T(8,128)(2,1)S(1)} %shard_map.103.mine_ref), channel_id=1, source_target_pairs={{0,8},{8,16},{16,24},{1,9},{9,17},{17,25},{2,10},{10,18},{18,26},{... | collective-permute-start | bytes 589832 | tf_op jit(solution)/shard_map/ppermute | solution.py:290
  25.1 8.5 %collective-permute-start.3 = (bf16[4,96,256]{2,1,0:T(8,128)(2,1)S(1)}, bf16[4,96,256]{2,1,0:T(8,128)(2,1)S(1)}, u32[]{:S(2)}, u32[]{:S(2)}) collective-permute-start(bf16[4,96,256]{2,1,0:T(8,128)(2,1)S(1)} %get-tuple-element.30), channel_id=1, source_target_pairs={{1,0},{2,1},{3,2},{4,3},{5,4},{6,5},{7,6},{9,8},{10,9},{11,10},{12... | collective-permute-start | bytes 589832 | tf_op jit(solution)/shard_map/ppermute | solution.py:290

commit v4 on v3

v4 whole, which is shorter than its diff:
```python
import jax
import jax.numpy as jnp
from jax import lax
from jax.experimental import pallas as pl
from jax.experimental.pallas import tpu as pltpu
from jax.sharding import PartitionSpec as P


F32 = jnp.float32
BF16 = jnp.bfloat16
VMEM = pl.BlockSpec(memory_space=pltpu.VMEM)
SMEM = pl.BlockSpec(memory_space=pltpu.SMEM)
HBM = pl.BlockSpec(memory_space=pltpu.HBM)


def silu_norm(values, gain):
    mean_sq = jnp.mean(values * values, axis=0, keepdims=True)
    scaled = values * lax.rsqrt(mean_sq + 1e-06) * gain
    return scaled / (1.0 + jnp.exp(-scaled))


def column_taps(act):
    lane = lax.broadcasted_iota(jnp.int32, act.shape, 1)
    width = act.shape[1]
    left = jnp.where(lane == 0, 0.0, pltpu.roll(act, 1, 1))
    right = jnp.where(lane == width - 1, 0.0, pltpu.roll(act, width - 1, 1))
    return left.astype(BF16), act.astype(BF16), right.astype(BF16)


def spread(vector, width):
    return jnp.broadcast_to(vector, (width, vector.shape[1])).T


def kept(clip_ref, frame, back):
    final = clip_ref.shape[0] - 1
    here = clip_ref[jnp.clip(frame, 0, final)]
    there = clip_ref[jnp.clip(frame - back, 0, final)]
    return (frame - back >= 0) & (here == there)


def fold_taps(weight_ref, row_tap):
    return jnp.concatenate([weight_ref[t, row_tap, j] for t in range(3) for j in range(3)], axis=1)


def dot(a, b):
    return jnp.dot(a, b, preferred_element_type=F32)


def norm_frame(lat_ref, frame, rows, gain, xs_ref):
    _, chans, height, width = lat_ref.shape
    values = lat_ref[frame].reshape(chans, height * width)
    for n, r in enumerate(rows):
        act = silu_norm(values[:, r * width : (r + 1) * width].astype(F32), gain)
        for j, tap in enumerate(column_taps(act)):
            xs_ref[pl.ds((frame * 3 + j) * chans, chans), n * width : (n + 1) * width] = tap


def clear_last(xs_ref, depth):
    xs_ref[pl.ds(xs_ref.shape[0] - depth, depth), :] = jnp.zeros((depth, xs_ref.shape[1]), xs_ref.dtype)


def conv_frame(xs_ref, wt_ref, clip_ref, start, out, lag):
    depth = wt_ref.shape[1] // 3
    zero = xs_ref.shape[0] // depth - 1
    taps = [t for t in range(3) if 0 <= out - 2 + t + lag < zero]
    blocks = []
    for t in taps:
        block = out - 2 + t + lag
        if t < 2:
            block = jnp.where(kept(clip_ref, start + out, 2 - t), block, zero)
        blocks.append(xs_ref[pl.ds(pl.multiple_of(block * depth, depth), depth), :])
    first = taps[0] * depth
    spare = first % 128
    if spare:
        blocks.insert(0, xs_ref[pl.ds(zero * depth, spare), :])
    weight = wt_ref[:, first - spare : (taps[-1] + 1) * depth]
    outs = weight.shape[0] // 3
    y = dot(weight, blocks[0] if len(blocks) == 1 else jnp.concatenate(blocks, axis=0))
    return [y[i * outs : (i + 1) * outs] for i in range(3)]


def first_kernel(clip_hbm, lat_hbm, weight_hbm, gain_hbm, wt_ref, up_ref, edge_ref, lat_ref, xs_ref, weight_ref, gain_ref, clip_ref, sems):
    frames, chans, height, width = lat_ref.shape
    outs = weight_ref.shape[3]
    start = lax.axis_index("tm") * frames
    pairs = [(gain_hbm, gain_ref)] + [(lat_hbm.at[f], lat_ref.at[f]) for f in range(frames)]
    pairs += [(clip_hbm, clip_ref), (weight_hbm, weight_ref)]
    copies = [pltpu.make_async_copy(a, b, sems.at[n]) for n, (a, b) in enumerate(pairs)]
    for copy in copies:
        copy.start()
    clear_last(xs_ref, 3 * chans)
    copies[0].wait()
    gain = spread(gain_ref[...], width)
    for f in range(frames):
        copies[1 + f].wait()
        norm_frame(lat_ref, f, (height - 2, height - 1), gain, xs_ref)
    for copy in copies[1 + frames :]:
        copy.wait()
    for i in range(3):
        wt_ref[i * outs : (i + 1) * outs, :] = fold_taps(weight_ref, i)
    for out in range(frames + 2):
        y0, y1, y2 = conv_frame(xs_ref, wt_ref, clip_ref, start, out, 0)
        far = y0[:, :width] + y1[:, width:]
        up_ref[out, :, :width] = far.astype(BF16)
        up_ref[out, :, width:] = y0[:, width:].astype(BF16)
        edge_ref[out, :, :width] = y2[:, :width]
        edge_ref[out, :, width : 2 * width] = y1[:, :width] + y2[:, width:]
        edge_ref[out, :, 2 * width :] = far


def inner_rows(xs_ref, wt_ref, clip_ref, start, edge_ref, out, width):
    inner = xs_ref.shape[1] // width
    y0, y1, y2 = conv_frame(xs_ref, wt_ref, clip_ref, start, out, 0)
    rows = []
    for h in range(-1, inner + 2):
        total = None
        for tap, row in ((y0, h - 1), (y1, h), (y2, h + 1)):
            if 0 <= row < inner:
                term = tap[:, row * width : (row + 1) * width]
                total = term if total is None else total + term
        if h >= inner - 1:
            e = h - inner + 1
            term = edge_ref[out, :, e * width : (e + 1) * width]
            total = term if total is None else total + term
        rows.append(total)
    return rows


def inner_kernel(clip_ref, lat_ref, gain_ref, wt_ref, edge_ref, bias_ref, gain_mid_ref, part_ref, early_ref, xs_ref):
    frames, chans, height, width = lat_ref.shape
    start = lax.axis_index("tm") * frames
    gain = spread(gain_ref[...], width)
    bias, gain_mid = spread(bias_ref[...], width), spread(gain_mid_ref[...], width)
    clear_last(xs_ref, 3 * chans)
    for f in range(frames):
        norm_frame(lat_ref, f, range(height - 2), gain, xs_ref)
    for k in range(4):
        rows = inner_rows(xs_ref, wt_ref, clip_ref, start, edge_ref, frames - 2 + k, width)
        for h, total in enumerate(rows, -1):
            if h < 1:
                part_ref[k, :, (h + 1) * width : (h + 2) * width] = total
            else:
                if k < 2:
                    total = act_rows(total, h, height, bias, gain_mid)
                early_ref[k, :, (h - 1) * width : h * width] = total.astype(BF16)


def head_kernel(clip_ref, xs_ref, wt_ref, edge_ref, weight_ref, head_ref, w_ref):
    frames, outs, _ = head_ref.shape
    width = edge_ref.shape[2] // 3
    start = lax.axis_index("tm") * (edge_ref.shape[0] - 2)
    for i in range(3):
        w_ref[i * outs : (i + 1) * outs, :] = fold_taps(weight_ref, i)
    for out in range(frames):
        rows = inner_rows(xs_ref, wt_ref, clip_ref, start, edge_ref, out, width)
        for n, total in enumerate(rows):
            head_ref[out, :, n * width : (n + 1) * width] = total


def act_rows(total, h, height, bias, gain):
    hidden = (total + bias).astype(BF16).astype(F32)
    act = silu_norm(hidden, gain)
    if h == -1:
        return jnp.where(lax.axis_index("rows") > 0, act, 0.0)
    if h == height - 1:
        return jnp.where(lax.axis_index("rows") == lax.axis_size("rows") - 1, act, 0.0)
    return act


def late_kernel(part_ref, got_ref, bias_ref, gain_ref, late_ref):
    width = got_ref.shape[2] // 2
    frames = got_ref.shape[0] - 2
    bias, gain = spread(bias_ref[...], width), spread(gain_ref[...], width)
    for k in range(4):
        for h in (-1, 0):
            cols = pl.ds((h + 1) * width, width)
            total = part_ref[k, :, cols] + got_ref[frames - 2 + k, :, cols].astype(F32)
            if k < 2:
                total = act_rows(total, h, 0, bias, gain)
            late_ref[k, :, cols] = total.astype(BF16)


def act_taps(mine_ref, before_ref, sums, rows, height, bias, gain, frames, xs_ref):
    outs = mine_ref.shape[1]
    width = mine_ref.shape[2] // len(rows)
    for s in range(-2, frames):
        for n, h in enumerate(rows):
            cols = pl.ds(n * width, width)
            if s < 0:
                act = before_ref[s + 2, :, cols].astype(F32)
            elif s >= frames - 2:
                act = mine_ref[s - frames + 2, :, cols].astype(F32)
            else:
                total = sums(s, h)
                if s < 2:
                    total = total + before_ref[2 + s, :, cols].astype(F32)
                act = act_rows(total, h, height, bias, gain)
            for j, tap in enumerate(column_taps(act)):
                xs_ref[pl.ds(((s + 2) * 3 + j) * outs, outs), cols] = tap


def edge_kernel(clip_ref, head_ref, got_ref, mine_ref, before_ref, bias_ref, gain_ref, w_ref, down_ref, edge_ref, xs_ref):
    width = got_ref.shape[2] // 2
    frames = got_ref.shape[0] - 2
    start = lax.axis_index("tm") * frames
    bias, gain = spread(bias_ref[...], width), spread(gain_ref[...], width)

    def sums(s, h):
        cols = pl.ds((h + 1) * width, width)
        return head_ref[s, :, cols] + got_ref[s, :, cols].astype(F32)

    clear_last(xs_ref, w_ref.shape[0])
    act_taps(mine_ref, before_ref, sums, (-1, 0), 0, bias, gain, frames, xs_ref)
    for out in range(frames):
        y0, y1, y2 = conv_frame(xs_ref, w_ref, clip_ref, start, out, 2)
        down_ref[out, :, :width] = y2[:, :width].astype(BF16)
        down_ref[out, :, width:] = (y1[:, :width] + y2[:, width:]).astype(BF16)
        edge_ref[out, :, :width] = y0[:, :width] + y1[:, width:]
        edge_ref[out, :, width:] = y0[:, width:]


def body_kernel(clip_ref, head_ref, mine_ref, before_ref, w_ref, edge_ref, bias_ref, gain_ref, lat_ref, skip_ref, bias_mid_ref, skip_bias_ref, total_ref, xs_ref):
    frames, chans, height, width = lat_ref.shape
    start = lax.axis_index("tm") * frames
    bias, gain = spread(bias_ref[...], width), spread(gain_ref[...], width)
    shift = spread(bias_mid_ref[...] + skip_bias_ref[...], width)
    sums = lambda s, h: head_ref[s, :, (h + 1) * width : (h + 2) * width]
    clear_last(xs_ref, w_ref.shape[0])
    act_taps(mine_ref, before_ref, sums, range(1, height), height, bias, gain, frames, xs_ref)
    skip = skip_ref[...]
    for out in range(frames):
        y0, y1, y2 = conv_frame(xs_ref, w_ref, clip_ref, start, out, 2)
        short = dot(skip, lat_ref[out].reshape(chans, height * width))
        for r in range(height):
            cols = pl.ds(r * width, width)
            total = short[:, r * width : (r + 1) * width] + shift
            for tap, row in ((y0, r - 1), (y1, r), (y2, r + 1)):
                if 1 <= row < height:
                    total = total + tap[:, (row - 1) * width : row * width]
            if r < 2:
                total = total + edge_ref[out, :, cols]
            total_ref[out, :, cols] = total


def last_kernel(total_ref, below_ref, out_ref):
    frames, outs, height, width = out_ref.shape
    for f in range(frames):
        rows = [total_ref[f, :, r * width : (r + 1) * width] for r in range(height)]
        for n in range(2):
            rows[height - 2 + n] = rows[height - 2 + n] + below_ref[f, :, n * width : (n + 1) * width].astype(F32)
        out_ref[f] = jnp.concatenate(rows, axis=1).reshape(outs, height, width).astype(BF16)


def call(kernel, shapes, operands, flops, places=(), scratch=()):
    moved = sum(x.size * x.dtype.itemsize for x in operands) + sum(s.size * s.dtype.itemsize for s in shapes)
    single = len(shapes) == 1
    places = list(places) + [VMEM] * (len(operands) - len(places))
    return pl.pallas_call(
        kernel,
        out_shape=shapes[0] if single else tuple(shapes),
        in_specs=places,
        out_specs=VMEM if single else tuple(VMEM for _ in shapes),
        scratch_shapes=list(scratch),
        cost_estimate=pl.CostEstimate(flops=flops, bytes_accessed=moved, transcendentals=0),
        compiler_params=pltpu.CompilerParams(vmem_limit_bytes=20 << 20),
    )(*operands)


def moved_by(block, axis, distance):
    devices = range(lax.axis_size(axis))
    return lax.ppermute(block, axis, [(i, i + distance) for i in devices if i + distance in devices])


def shards(latent, clip_ids, gain_in, conv_in, bias_in, gain_mid, conv_mid, bias_mid, skip_weight, skip_bias):
    frames, chans, height, width = latent.shape
    outs = conv_in.shape[3]
    shape = jax.ShapeDtypeStruct
    row = lambda v: v.reshape(1, -1)
    deep, deep_mid, tall = 3 * chans, 3 * outs, 3 * outs
    work = 2 * tall * 3 * deep * frames * width
    wt, up, edge, lat = call(
        first_kernel,
        [
            shape((tall, 3 * deep), BF16),
            shape((frames + 2, outs, 2 * width), BF16),
            shape((frames + 2, outs, 3 * width), F32),
            shape(latent.shape, BF16),
        ],
        tuple(pltpu.with_memory_space_constraint(x, pltpu.HBM) for x in (clip_ids, latent, conv_in, row(gain_in))),
        work * 2,
        [HBM] * 4,
        [
            pltpu.VMEM(((frames + 1) * deep, 2 * width), BF16),
            pltpu.VMEM(conv_in.shape, BF16),
            pltpu.VMEM((1, chans), F32),
            pltpu.SMEM(clip_ids.shape, jnp.int32),
            pltpu.SemaphoreType.DMA((frames + 3,)),
        ],
    )
    got = moved_by(up, "rows", 1)
    part, early, xs = call(
        inner_kernel,
        [
            shape((4, outs, 2 * width), F32),
            shape((4, outs, (height - 1) * width), BF16),
            shape(((frames + 1) * deep, (height - 2) * width), BF16),
        ],
        (clip_ids, lat, row(gain_in), wt, edge, row(bias_in), row(gain_mid)),
        work * (height - 2),
        [SMEM],
    )
    before_early = moved_by(early, "tm", 1)
    head, w_mid = call(
        head_kernel,
        [shape((frames - 2, outs, (height + 1) * width), F32), shape((tall, 3 * deep_mid), BF16)],
        (clip_ids, xs, wt, edge, conv_mid),
        work,
        [SMEM],
    )
    late = call(
        late_kernel,
        [shape((4, outs, 2 * width), BF16)],
        (part, got, row(bias_in), row(gain_mid)),
        1000,
    )
    before_late = moved_by(late, "tm", 1)
    down, edge_mid = call(
        edge_kernel,
        [shape((frames, outs, 2 * width), BF16), shape((frames, outs, 2 * width), F32)],
        (clip_ids, head, got, late, before_late, row(bias_in), row(gain_mid), w_mid),
        work,
        [SMEM],
        [pltpu.VMEM(((frames + 3) * deep_mid, 2 * width), BF16)],
    )
    below = moved_by(down, "rows", -1)
    total = call(
        body_kernel,
        [shape((frames, outs, height * width), F32)],
        (clip_ids, head, early, before_early, w_mid, edge_mid, row(bias_in), row(gain_mid), lat, skip_weight, row(bias_mid), row(skip_bias)),
        work * (height - 1) // 2,
        [SMEM],
        [pltpu.VMEM(((frames + 3) * deep_mid, (height - 1) * width), BF16)],
    )
    return call(last_kernel, [shape((frames, outs, height, width), BF16)], (total, below), 1000)


def solution(mesh):
    return jax.shard_map(
        shards,
        mesh=mesh,
        in_specs=(P("tm", None, "rows", None), P(), P(), P(), P(), P(), P(), P(), P(), P()),
        out_specs=P("tm", None, "rows", None),
        check_vma=False,
    )
```

time: 34.9 us -> 33.9 us (0.971)
  the two profiles are of different devices: /device:TPU:22 before, /device:TPU:0 now
where the time goes in v4:
time: 33.9 us; the launch traced here: 33.7 us
  Pallas kernels  12.5 us (37%)
  starting transfers between devices  11.6 us (34%)
  waiting for transfers between devices  9.37 us (28%)
    pallas_call x7, Pallas kernels, call(): pl.pallas_call(kernel, out_shape=shapes[0] if single else tuple(shapes),...  12.5 us
    ppermute x4, starting transfers between devices, moved_by(): lax.ppermute(block, axis, [(i, i + distance) for i in devices if i + dist...  11.6 us
    ppermute x4, waiting for transfers between devices, moved_by(): lax.ppermute(block, axis, [(i, i + distance) for i in devices if i + dist...  9.37 us
  transfers between devices with their start and end apart: 4, of which 2 were waited for; matrix products, arithmetic and copies ran while one was open for 0% of the time, Pallas kernels for 23%

profile of v4, /device:TPU:0, one launch (start us, length us, event | category | flops | bytes accessed | tf_op | source)
XLA Modules:
  0.0 33.7 jit_solution(9839396637709332399)
XLA Ops:
  0.0 0.0 copy-start.2
  0.0 0.0 copy-start.3
  0.0 0.0 copy-start.4
  0.0 0.0 copy-start.7
  0.0 3.7 %shard_map.100 = (bf16[288,1728]{1,0:T(8,128)(2,1)S(1)}, bf16[6,96,256]{2,1,0:T(8,128)(2,1)S(1)}, f32[6,96,384]{2,1,0:T(8,128)S(1)}, bf16[4,192,4,128]{3,2,1,0:T(4,128)(2,1)S(1)}) custom-call(s32[16]{0:T(128)} %clip_ref.7, bf16[4,192,4,128]{3,2,1,0:T(4,128)(2,1)} %lat_hbm.1, bf16[3,3,3,96,192]{4,3,2,1,0:T(8,128)(2,1)} %weight_hbm.1, f32[1,192]{1,0:T(1,128)} %bitcast.15), custom_call_target="tpu_custom_call" | custom-call | flops 1019215872 | bytes 4744000 | tf_op jit(solution)/shard_map/pallas_call | solution.py:258
  3.7 4.9 %collective-permute-start.1 = (bf16[6,96,256]{2,1,0:T(8,128)(2,1)S(1)}, bf16[6,96,256]{2,1,0:T(8,128)(2,1)S(1)}, u32[]{:S(2)}, u32[]{:S(2)}) collective-permute-start(bf16[6,96,256]{2,1,0:T(8,128)(2,1)S(1)} %get-tuple-element.23), channel_id=1, source_target_pairs={{0,1},{1,2},{2,3},{3,4},{4,5},{5,6},{6,7},{8,9},{9,10},{10,11},{11... | collective-permute-start | bytes 884744 | tf_op jit(solution)/shard_map/ppermute | solution.py:271
  8.6 0.0 copy-done.2
  8.6 0.0 copy-done.3
  8.6 0.0 copy-done.4
  8.6 0.0 copy-done.7
  8.7 0.0 copy-start
  8.7 2.4 %shard_map.101 = (f32[4,96,256]{2,1,0:T(8,128)S(1)}, bf16[4,96,384]{2,1,0:T(8,128)(2,1)S(1)}, bf16[2880,256]{1,0:T(8,128)(2,1)S(1)}) custom-call(s32[16]{0:T(128)S(1)} %copy-done.2, bf16[4,192,4,128]{3,2,1,0:T(4,128)(2,1)S(1)} %get-tuple-element.16.lat_ref, f32[1,192]{1,0:T(1,128)S(1)} %bitcast.16, bf16[288,1728]{1,0:T(8,128)(2,1)S(1)} %get-tuple-element.17.wt_ref, ...), custom_call_target="tpu_custom_call" | custom-call | flops 1019215872 | bytes 4830784 | tf_op jit(solution)/shard_map/pallas_call | solution.py:258
  11.1 3.8 %collective-permute-done.1.got_ref = bf16[6,96,256]{2,1,0:T(8,128)(2,1)S(1)} collective-permute-done((bf16[6,96,256]{2,1,0:T(8,128)(2,1)S(1)}, bf16[6,96,256]{2,1,0:T(8,128)(2,1)S(1)}, u32[]{:S(2)}, u32[]{:S(2)}) %collective-permute-start.1) | collective-permute-done | bytes 294944 | tf_op jit(solution)/shard_map/ppermute | solution.py:271
  14.8 0.2 shard_map.103.mine_ref
  15.1 1.3 %collective-permute-start.2 = (bf16[4,96,256]{2,1,0:T(8,128)(2,1)S(1)}, bf16[4,96,256]{2,1,0:T(8,128)(2,1)S(1)}, u32[]{:S(2)}, u32[]{:S(2)}) collective-permute-start(bf16[4,96,256]{2,1,0:T(8,128)(2,1)S(1)} %shard_map.103.mine_ref), channel_id=1, source_target_pairs={{0,8},{8,16},{16,24},{1,9},{9,17},{17,25},{2,10},{10,18},{18,26},{... | collective-permute-start | bytes 589832 | tf_op jit(solution)/shard_map/ppermute | solution.py:271
  16.4 4.1 %collective-permute-start = (bf16[4,96,384]{2,1,0:T(8,128)(2,1)S(1)}, bf16[4,96,384]{2,1,0:T(8,128)(2,1)S(1)}, u32[]{:S(2)}, u32[]{:S(2)}) collective-permute-start(bf16[4,96,384]{2,1,0:T(8,128)(2,1)S(1)} %get-tuple-element.21.mine_ref), channel_id=1, source_target_pairs={{0,8},{8,16},{16,24},{1,9},{9,17},{17,25},{2,10},{10,18},{18,26},{... | collective-permute-start | bytes 884744 | tf_op jit(solution)/shard_map/ppermute | solution.py:271
  20.5 0.0 copy-done
  20.5 1.0 %shard_map.102 = (f32[2,96,640]{2,1,0:T(8,128)S(1)}, bf16[288,864]{1,0:T(8,128)(2,1)S(1)}) custom-call(s32[16]{0:T(128)S(1)} %copy-done.2, bf16[2880,256]{1,0:T(8,128)(2,1)S(1)} %get-tuple-element.19.xs_ref, bf16[288,1728]{1,0:T(8,128)(2,1)S(1)} %get-tuple-element.17.wt_ref, f32[6,96,384]{2,1,0:T(8,128)S(1)} %get-tuple-element.18.edge_ref, ...), custom_call_target="tpu_custom_call" | custom-call | flops 509607936 | bytes 4841536 | tf_op jit(solution)/shard_map/pallas_call | solution.py:258
  21.6 0.0 copy-start.1
  21.6 0.0 copy-start.5
  21.6 0.0 copy-start.6
  21.6 0.0 collective-permute-done.2.before_ref
  21.6 1.7 %shard_map.104 = (bf16[4,96,256]{2,1,0:T(8,128)(2,1)S(1)}, f32[4,96,256]{2,1,0:T(8,128)S(1)}) custom-call(s32[16]{0:T(128)S(1)} %copy-done.2, f32[2,96,640]{2,1,0:T(8,128)S(1)} %get-tuple-element.20.head_ref, bf16[6,96,256]{2,1,0:T(8,128)(2,1)S(1)} %collective-permute-done.1.got_ref, bf16[4,96,256]{2,1,0:T(8,128)(2,1)S(1)} %shard_map.103.mine_ref, ...), custom_call_target="tpu_custom_call" | custom-call | flops 509607936 | bytes 2267968 | tf_op jit(solution)/shard_map/pallas_call | solution.py:258
  23.3 1.3 %collective-permute-start.3 = (bf16[4,96,256]{2,1,0:T(8,128)(2,1)S(1)}, bf16[4,96,256]{2,1,0:T(8,128)(2,1)S(1)}, u32[]{:S(2)}, u32[]{:S(2)}) collective-permute-start(bf16[4,96,256]{2,1,0:T(8,128)(2,1)S(1)} %get-tuple-element.26), channel_id=1, source_target_pairs={{1,0},{2,1},{3,2},{4,3},{5,4},{6,5},{7,6},{9,8},{10,9},{11,10},{12... | collective-permute-start | bytes 589832 | tf_op jit(solution)/shard_map/ppermute | solution.py:271
  24.6 0.0 collective-permute-done.before_ref
  24.6 0.0 copy-done.1
  24.6 0.0 copy-done.5
  24.6 0.0 copy-done.6
  24.7 2.5 %shard_map.105.total_ref = f32[4,96,512]{2,1,0:T(8,128)S(1)} custom-call(s32[16]{0:T(128)S(1)} %copy-done.2, f32[2,96,640]{2,1,0:T(8,128)S(1)} %get-tuple-element.20.head_ref, bf16[4,96,384]{2,1,0:T(8,128)(2,1)S(1)} %get-tuple-element.21.mine_ref, bf16[4,96,384]{2,1,0:T(8,128)(2,1)S(1)} %collective-permute-done.before_ref, ...), custom_call_target="tpu_custom_call" | custom-call | flops 764411904 | bytes 3583552 | tf_op jit(solution)/shard_map/pallas_call | solution.py:258
  27.2 5.6 %collective-permute-done.3.below_ref = bf16[4,96,256]{2,1,0:T(8,128)(2,1)S(1)} collective-permute-done((bf16[4,96,256]{2,1,0:T(8,128)(2,1)S(1)}, bf16[4,96,256]{2,1,0:T(8,128)(2,1)S(1)}, u32[]{:S(2)}, u32[]{:S(2)}) %collective-permute-start.3) | collective-permute-done | bytes 196640 | tf_op jit(solution)/shard_map/ppermute | solution.py:271
  32.8 1.0 %shard_map.106 = bf16[4,96,4,128]{3,2,1,0:T(4,128)(2,1)} custom-call(f32[4,96,512]{2,1,0:T(8,128)S(1)} %shard_map.105.total_ref, bf16[4,96,256]{2,1,0:T(8,128)(2,1)S(1)} %collective-permute-done.3.below_ref), custom_call_target="tpu_custom_call" | custom-call | flops 1000 | bytes 1376256 | tf_op jit(solution)/shard_map/pallas_call | solution.py:258
Async XLA Ops:
  0.0 8.6 %copy-start.2 = (s32[16]{0:T(128)S(1)}, s32[16]{0:T(128)}, u32[]{:S(2)}) copy-start(s32[16]{0:T(128)} %clip_ref.7) | copy-start | bytes 196
  0.0 8.6 %copy-start.3 = (f32[96]{0:T(128)S(1)}, f32[96]{0:T(128)}, u32[]{:S(2)}) copy-start(f32[96]{0:T(128)} %param.14) | copy-start | bytes 1156
  0.0 8.6 %copy-start.4 = (f32[96]{0:T(128)S(1)}, f32[96]{0:T(128)}, u32[]{:S(2)}) copy-start(f32[96]{0:T(128)} %param.15) | copy-start | bytes 1156
  0.0 8.6 %copy-start.7 = (f32[192]{0:T(256)S(1)}, f32[192]{0:T(256)}, u32[]{:S(2)}) copy-start(f32[192]{0:T(256)} %param.12) | copy-start | bytes 2308
  3.7 11.2 %collective-permute-start.1 = (bf16[6,96,256]{2,1,0:T(8,128)(2,1)S(1)}, bf16[6,96,256]{2,1,0:T(8,128)(2,1)S(1)}, u32[]{:S(2)}, u32[]{:S(2)}) collective-permute-start(bf16[6,96,256]{2,1,0:T(8,128)(2,1)S(1)} %get-tuple-element.23), channel_id=1, source_target_pairs={{0,1},{1,2},{2,3},{3,4},{4,5},{5,6},{6,7},{8,9},{9,10},{10,11},{11... | collective-permute-start | bytes 884744 | tf_op jit(solution)/shard_map/ppermute | solution.py:271
  8.7 11.9 %copy-start = (bf16[3,3,3,96,96]{4,3,2,1,0:T(8,128)(2,1)S(1)}, bf16[3,3,3,96,96]{4,3,2,1,0:T(8,128)(2,1)}, u32[]{:S(2)}) copy-start(bf16[3,3,3,96,96]{4,3,2,1,0:T(8,128)(2,1)} %weight_ref.1) | copy-start | bytes 1492996
  15.1 6.6 %collective-permute-start.2 = (bf16[4,96,256]{2,1,0:T(8,128)(2,1)S(1)}, bf16[4,96,256]{2,1,0:T(8,128)(2,1)S(1)}, u32[]{:S(2)}, u32[]{:S(2)}) collective-permute-start(bf16[4,96,256]{2,1,0:T(8,128)(2,1)S(1)} %shard_map.103.mine_ref), channel_id=1, source_target_pairs={{0,8},{8,16},{16,24},{1,9},{9,17},{17,25},{2,10},{10,18},{18,26},{... | collective-permute-start | bytes 589832 | tf_op jit(solution)/shard_map/ppermute | solution.py:271
  16.4 8.3 %collective-permute-start = (bf16[4,96,384]{2,1,0:T(8,128)(2,1)S(1)}, bf16[4,96,384]{2,1,0:T(8,128)(2,1)S(1)}, u32[]{:S(2)}, u32[]{:S(2)}) collective-permute-start(bf16[4,96,384]{2,1,0:T(8,128)(2,1)S(1)} %get-tuple-element.21.mine_ref), channel_id=1, source_target_pairs={{0,8},{8,16},{16,24},{1,9},{9,17},{17,25},{2,10},{10,18},{18,26},{... | collective-permute-start | bytes 884744 | tf_op jit(solution)/shard_map/ppermute | solution.py:271
  21.6 3.1 %copy-start.1 = (bf16[96,192]{1,0:T(8,128)(2,1)S(1)}, bf16[96,192]{1,0:T(8,128)(2,1)}, u32[]{:S(2)}) copy-start(bf16[96,192]{1,0:T(8,128)(2,1)} %skip_ref.1) | copy-start | bytes 110596
  21.6 3.1 %copy-start.5 = (f32[96]{0:T(128)S(1)}, f32[96]{0:T(128)}, u32[]{:S(2)}) copy-start(f32[96]{0:T(128)} %param.17) | copy-start | bytes 1156
  21.6 3.1 %copy-start.6 = (f32[96]{0:T(128)S(1)}, f32[96]{0:T(128)}, u32[]{:S(2)}) copy-start(f32[96]{0:T(128)} %param.19) | copy-start | bytes 1156
  23.3 9.5 %collective-permute-start.3 = (bf16[4,96,256]{2,1,0:T(8,128)(2,1)S(1)}, bf16[4,96,256]{2,1,0:T(8,128)(2,1)S(1)}, u32[]{:S(2)}, u32[]{:S(2)}) collective-permute-start(bf16[4,96,256]{2,1,0:T(8,128)(2,1)S(1)} %get-tuple-element.26), channel_id=1, source_target_pairs={{1,0},{2,1},{3,2},{4,3},{5,4},{6,5},{7,6},{9,8},{10,9},{11,10},{12... | collective-permute-start | bytes 589832 | tf_op jit(solution)/shard_map/ppermute | solution.py:271

commit v5 on v4

--- a/solution.py
+++ b/solution.py
@@ -9,7 +9,6 @@
 F32 = jnp.float32
 BF16 = jnp.bfloat16
 VMEM = pl.BlockSpec(memory_space=pltpu.VMEM)
-SMEM = pl.BlockSpec(memory_space=pltpu.SMEM)
 HBM = pl.BlockSpec(memory_space=pltpu.HBM)
 
 
@@ -38,8 +37,8 @@
     return (frame - back >= 0) & (here == there)
 
 
-def fold_taps(weight_ref, row_tap):
-    return jnp.concatenate([weight_ref[t, row_tap, j] for t in range(3) for j in range(3)], axis=1)
+def fold_taps(weight_ref, row_tap, taps):
+    return jnp.concatenate([weight_ref[t, row_tap, j] for t in taps for j in range(3)], axis=1)
 
 
 def dot(a, b):
@@ -55,51 +54,51 @@
             xs_ref[pl.ds((frame * 3 + j) * chans, chans), n * width : (n + 1) * width] = tap
 
 
-def clear_last(xs_ref, depth):
-    xs_ref[pl.ds(xs_ref.shape[0] - depth, depth), :] = jnp.zeros((depth, xs_ref.shape[1]), xs_ref.dtype)
-
-
-def conv_frame(xs_ref, wt_ref, clip_ref, start, out, lag):
+def conv_frame(xs_ref, wt_ref, keep_ref, out, lag):
     depth = wt_ref.shape[1] // 3
-    zero = xs_ref.shape[0] // depth - 1
-    taps = [t for t in range(3) if 0 <= out - 2 + t + lag < zero]
+    columns = xs_ref.shape[1]
+    taps = [t for t in range(3) if 0 <= out - 2 + t + lag < xs_ref.shape[0] // depth]
     blocks = []
     for t in taps:
-        block = out - 2 + t + lag
+        block = xs_ref[pl.ds((out - 2 + t + lag) * depth, depth), :]
         if t < 2:
-            block = jnp.where(kept(clip_ref, start + out, 2 - t), block, zero)
-        blocks.append(xs_ref[pl.ds(pl.multiple_of(block * depth, depth), depth), :])
+            keep = keep_ref[2 * out + 1 - t]
+            high, width = keep.shape
+            keep = jnp.concatenate([keep] * (columns // width), axis=1)
+            block = (block.reshape(depth // high, high, columns) * keep[None]).reshape(depth, columns)
+        blocks.append(block)
     first = taps[0] * depth
     spare = first % 128
     if spare:
-        blocks.insert(0, xs_ref[pl.ds(zero * depth, spare), :])
+        blocks.insert(0, jnp.zeros((spare, columns), BF16))
     weight = wt_ref[:, first - spare : (taps[-1] + 1) * depth]
     outs = weight.shape[0] // 3
     y = dot(weight, blocks[0] if len(blocks) == 1 else jnp.concatenate(blocks, axis=0))
     return [y[i * outs : (i + 1) * outs] for i in range(3)]
 
 
-def first_kernel(clip_hbm, lat_hbm, weight_hbm, gain_hbm, wt_ref, up_ref, edge_ref, lat_ref, xs_ref, weight_ref, gain_ref, clip_ref, sems):
-    frames, chans, height, width = lat_ref.shape
+def first_kernel(clip_hbm, lat_hbm, weight_hbm, gain_hbm, wt_ref, up_ref, edge_ref, lat_ref, keep_ref, xs_ref, weight_ref, gain_ref, clip_ref, sems):
+    frames, _, height, width = lat_ref.shape
     outs = weight_ref.shape[3]
     start = lax.axis_index("tm") * frames
-    pairs = [(gain_hbm, gain_ref)] + [(lat_hbm.at[f], lat_ref.at[f]) for f in range(frames)]
-    pairs += [(clip_hbm, clip_ref), (weight_hbm, weight_ref)]
+    pairs = [(gain_hbm, gain_ref)] + [(lat_hbm.at[f], lat_ref.at[f]) for f in range(frames)] + [(clip_hbm, clip_ref)]
+    pairs += [(weight_hbm, weight_ref)]
     copies = [pltpu.make_async_copy(a, b, sems.at[n]) for n, (a, b) in enumerate(pairs)]
     for copy in copies:
         copy.start()
-    clear_last(xs_ref, 3 * chans)
     copies[0].wait()
     gain = spread(gain_ref[...], width)
     for f in range(frames):
         copies[1 + f].wait()
         norm_frame(lat_ref, f, (height - 2, height - 1), gain, xs_ref)
-    for copy in copies[1 + frames :]:
-        copy.wait()
-    for i in range(3):
-        wt_ref[i * outs : (i + 1) * outs, :] = fold_taps(weight_ref, i)
+    copies[1 + frames].wait()
     for out in range(frames + 2):
-        y0, y1, y2 = conv_frame(xs_ref, wt_ref, clip_ref, start, out, 0)
+        for back in (1, 2):
+            flag = jnp.where(kept(clip_ref, start + out, back), 1.0, 0.0)
+            keep_ref[2 * out + back - 1] = jnp.full(keep_ref.shape[1:], flag, F32).astype(BF16)
+
+    def message(out):
+        y0, y1, y2 = conv_frame(xs_ref, wt_ref, keep_ref, out, 0)
         far = y0[:, :width] + y1[:, width:]
         up_ref[out, :, :width] = far.astype(BF16)
         up_ref[out, :, width:] = y0[:, width:].astype(BF16)
@@ -107,10 +106,17 @@
         edge_ref[out, :, width : 2 * width] = y1[:, :width] + y2[:, width:]
         edge_ref[out, :, 2 * width :] = far
 
-
-def inner_rows(xs_ref, wt_ref, clip_ref, start, edge_ref, out, width):
+    for copy in copies[2 + frames :]:
+        copy.wait()
+    for i in range(3):
+        wt_ref[i * outs : (i + 1) * outs, :] = fold_taps(weight_ref, i, range(3))
+    for out in range(frames + 2):
+        message(out)
+
+
+def inner_rows(xs_ref, wt_ref, keep_ref, edge_ref, out, width):
     inner = xs_ref.shape[1] // width
-    y0, y1, y2 = conv_frame(xs_ref, wt_ref, clip_ref, start, out, 0)
+    y0, y1, y2 = conv_frame(xs_ref, wt_ref, keep_ref, out, 0)
     rows = []
     for h in range(-1, inner + 2):
         total = None
@@ -126,16 +132,16 @@
     return rows
 
 
-def inner_kernel(clip_ref, lat_ref, gain_ref, wt_ref, edge_ref, bias_ref, gain_mid_ref, part_ref, early_ref, xs_ref):
-    frames, chans, height, width = lat_ref.shape
-    start = lax.axis_index("tm") * frames
+def inner_kernel(keep_ref, lat_ref, gain_ref, wt_ref, edge_ref, bias_ref, gain_mid_ref, part_ref, early_ref, xs_ref, mid_ref):
+    frames, _, height, width = lat_ref.shape
     gain = spread(gain_ref[...], width)
     bias, gain_mid = spread(bias_ref[...], width), spread(gain_mid_ref[...], width)
-    clear_last(xs_ref, 3 * chans)
+    mid_ref[0] = bias
+    mid_ref[1] = gain_mid
     for f in range(frames):
         norm_frame(lat_ref, f, range(height - 2), gain, xs_ref)
     for k in range(4):
-        rows = inner_rows(xs_ref, wt_ref, clip_ref, start, edge_ref, frames - 2 + k, width)
+        rows = inner_rows(xs_ref, wt_ref, keep_ref, edge_ref, frames - 2 + k, width)
         for h, total in enumerate(rows, -1):
             if h < 1:
                 part_ref[k, :, (h + 1) * width : (h + 2) * width] = total
@@ -145,14 +151,13 @@
                 early_ref[k, :, (h - 1) * width : h * width] = total.astype(BF16)
 
 
-def head_kernel(clip_ref, xs_ref, wt_ref, edge_ref, weight_ref, head_ref, w_ref):
+def head_kernel(keep_ref, xs_ref, wt_ref, edge_ref, weight_ref, head_ref, w_ref):
     frames, outs, _ = head_ref.shape
     width = edge_ref.shape[2] // 3
-    start = lax.axis_index("tm") * (edge_ref.shape[0] - 2)
     for i in range(3):
-        w_ref[i * outs : (i + 1) * outs, :] = fold_taps(weight_ref, i)
+        w_ref[i * outs : (i + 1) * outs, :] = fold_taps(weight_ref, i, range(3))
     for out in range(frames):
-        rows = inner_rows(xs_ref, wt_ref, clip_ref, start, edge_ref, out, width)
+        rows = inner_rows(xs_ref, wt_ref, keep_ref, edge_ref, out, width)
         for n, total in enumerate(rows):
             head_ref[out, :, n * width : (n + 1) * width] = total
 
@@ -167,10 +172,10 @@
     return act
 
 
-def late_kernel(part_ref, got_ref, bias_ref, gain_ref, late_ref):
+def late_kernel(part_ref, got_ref, mid_ref, late_ref):
     width = got_ref.shape[2] // 2
     frames = got_ref.shape[0] - 2
-    bias, gain = spread(bias_ref[...], width), spread(gain_ref[...], width)
+    bias, gain = mid_ref[0], mid_ref[1]
     for k in range(4):
         for h in (-1, 0):
             cols = pl.ds((h + 1) * width, width)
@@ -199,37 +204,33 @@
                 xs_ref[pl.ds(((s + 2) * 3 + j) * outs, outs), cols] = tap
 
 
-def edge_kernel(clip_ref, head_ref, got_ref, mine_ref, before_ref, bias_ref, gain_ref, w_ref, down_ref, edge_ref, xs_ref):
+def edge_kernel(keep_ref, head_ref, got_ref, mine_ref, before_ref, mid_ref, w_ref, down_ref, edge_ref, xs_ref):
     width = got_ref.shape[2] // 2
     frames = got_ref.shape[0] - 2
-    start = lax.axis_index("tm") * frames
-    bias, gain = spread(bias_ref[...], width), spread(gain_ref[...], width)
+    bias, gain = mid_ref[0], mid_ref[1]
 
     def sums(s, h):
         cols = pl.ds((h + 1) * width, width)
         return head_ref[s, :, cols] + got_ref[s, :, cols].astype(F32)
 
-    clear_last(xs_ref, w_ref.shape[0])
     act_taps(mine_ref, before_ref, sums, (-1, 0), 0, bias, gain, frames, xs_ref)
     for out in range(frames):
-        y0, y1, y2 = conv_frame(xs_ref, w_ref, clip_ref, start, out, 2)
+        y0, y1, y2 = conv_frame(xs_ref, w_ref, keep_ref, out, 2)
         down_ref[out, :, :width] = y2[:, :width].astype(BF16)
         down_ref[out, :, width:] = (y1[:, :width] + y2[:, width:]).astype(BF16)
         edge_ref[out, :, :width] = y0[:, :width] + y1[:, width:]
         edge_ref[out, :, width:] = y0[:, width:]
 
 
-def body_kernel(clip_ref, head_ref, mine_ref, before_ref, w_ref, edge_ref, bias_ref, gain_ref, lat_ref, skip_ref, bias_mid_ref, skip_bias_ref, total_ref, xs_ref):
+def body_kernel(keep_ref, head_ref, mine_ref, before_ref, w_ref, edge_ref, mid_ref, lat_ref, skip_ref, bias_mid_ref, skip_bias_ref, total_ref, xs_ref):
     frames, chans, height, width = lat_ref.shape
-    start = lax.axis_index("tm") * frames
-    bias, gain = spread(bias_ref[...], width), spread(gain_ref[...], width)
+    bias, gain = mid_ref[0], mid_ref[1]
     shift = spread(bias_mid_ref[...] + skip_bias_ref[...], width)
     sums = lambda s, h: head_ref[s, :, (h + 1) * width : (h + 2) * width]
-    clear_last(xs_ref, w_ref.shape[0])
     act_taps(mine_ref, before_ref, sums, range(1, height), height, bias, gain, frames, xs_ref)
     skip = skip_ref[...]
     for out in range(frames):
-        y0, y1, y2 = conv_frame(xs_ref, w_ref, clip_ref, start, out, 2)
+        y0, y1, y2 = conv_frame(xs_ref, w_ref, keep_ref, out, 2)
         short = dot(skip, lat_ref[out].reshape(chans, height * width))
         for r in range(height):
             cols = pl.ds(r * width, width)
@@ -278,19 +279,20 @@
     row = lambda v: v.reshape(1, -1)
     deep, deep_mid, tall = 3 * chans, 3 * outs, 3 * outs
     work = 2 * tall * 3 * deep * frames * width
-    wt, up, edge, lat = call(
+    wt, up, edge, lat, keep = call(
         first_kernel,
         [
             shape((tall, 3 * deep), BF16),
             shape((frames + 2, outs, 2 * width), BF16),
             shape((frames + 2, outs, 3 * width), F32),
             shape(latent.shape, BF16),
+            shape((2 * (frames + 2), 16, width), BF16),
         ],
         tuple(pltpu.with_memory_space_constraint(x, pltpu.HBM) for x in (clip_ids, latent, conv_in, row(gain_in))),
         work * 2,
         [HBM] * 4,
         [
-            pltpu.VMEM(((frames + 1) * deep, 2 * width), BF16),
+            pltpu.VMEM((frames * deep, 2 * width), BF16),
             pltpu.VMEM(conv_in.shape, BF16),
             pltpu.VMEM((1, chans), F32),
             pltpu.SMEM(clip_ids.shape, jnp.int32),
@@ -298,48 +300,40 @@
         ],
     )
     got = moved_by(up, "rows", 1)
-    part, early, xs = call(
+    part, early, xs, mid = call(
         inner_kernel,
         [
             shape((4, outs, 2 * width), F32),
             shape((4, outs, (height - 1) * width), BF16),
-            shape(((frames + 1) * deep, (height - 2) * width), BF16),
+            shape((frames * deep, (height - 2) * width), BF16),
+            shape((2, outs, width), F32),
         ],
-        (clip_ids, lat, row(gain_in), wt, edge, row(bias_in), row(gain_mid)),
+        (keep, lat, row(gain_in), wt, edge, row(bias_in), row(gain_mid)),
         work * (height - 2),
-        [SMEM],
     )
     before_early = moved_by(early, "tm", 1)
     head, w_mid = call(
         head_kernel,
         [shape((frames - 2, outs, (height + 1) * width), F32), shape((tall, 3 * deep_mid), BF16)],
-        (clip_ids, xs, wt, edge, conv_mid),
+        (keep, xs, wt, edge, conv_mid),
         work,
-        [SMEM],
-    )
-    late = call(
-        late_kernel,
-        [shape((4, outs, 2 * width), BF16)],
-        (part, got, row(bias_in), row(gain_mid)),
-        1000,
-    )
+    )
+    late = call(late_kernel, [shape((4, outs, 2 * width), BF16)], (part, got, mid), 1000)
     before_late = moved_by(late, "tm", 1)
     down, edge_mid = call(
         edge_kernel,
         [shape((frames, outs, 2 * width), BF16), shape((frames, outs, 2 * width), F32)],
-        (clip_ids, head, got, late, before_late, row(bias_in), row(gain_mid), w_mid),
+        (keep, head, got, late, before_late, mid, w_mid),
         work,
-        [SMEM],
-        [pltpu.VMEM(((frames + 3) * deep_mid, 2 * width), BF16)],
+        scratch=[pltpu.VMEM(((frames + 2) * deep_mid, 2 * width), BF16)],
     )
     below = moved_by(down, "rows", -1)
     total = call(
         body_kernel,
         [shape((frames, outs, height * width), F32)],
-        (clip_ids, head, early, before_early, w_mid, edge_mid, row(bias_in), row(gain_mid), lat, skip_weight, row(bias_mid), row(skip_bias)),
+        (keep, head, early, before_early, w_mid, edge_mid, mid, lat, skip_weight, row(bias_mid), row(skip_bias)),
         work * (height - 1) // 2,
-        [SMEM],
-        [pltpu.VMEM(((frames + 3) * deep_mid, (height - 1) * width), BF16)],
+        scratch=[pltpu.VMEM(((frames + 2) * deep_mid, (height - 1) * width), BF16)],
     )
     return call(last_kernel, [shape((frames, outs, height, width), BF16)], (total, below), 1000)
 

time: 33.9 us -> 32.7 us (0.965)
  Pallas kernels: 12.5 us -> 9.75 us
  waiting for transfers between devices: 9.37 us -> 10.9 us
    pallas_call x7, Pallas kernels: 12.5 us -> 9.75 us  [call(): pl.pallas_call(kernel, out_shape=shapes[0] if single else tuple(shapes),...]
    ppermute x4, waiting for transfers between devices: 9.37 us -> 10.9 us  [moved_by(): lax.ppermute(block, axis, [(i, i + distance) for i in devices if i + dist...]
  transfers between devices with their start and end apart: 4 -> 4, of which waited for: 2 -> 2; matrix products, arithmetic and copies ran while one was open for 0% -> 0% of each run, Pallas kernels for 23% -> 15%
where the time goes in v5:
time: 32.7 us; the launch traced here: 32.5 us
  starting transfers between devices  11.6 us (35%)
  waiting for transfers between devices  10.9 us (33%)
  Pallas kernels  9.75 us (30%)
    ppermute x4, starting transfers between devices, moved_by(): lax.ppermute(block, axis, [(i, i + distance) for i in devices if i + dist...  11.6 us
    ppermute x4, waiting for transfers between devices, moved_by(): lax.ppermute(block, axis, [(i, i + distance) for i in devices if i + dist...  10.9 us
    pallas_call x7, Pallas kernels, call(): pl.pallas_call(kernel, out_shape=shapes[0] if single else tuple(shapes),...  9.75 us
  transfers between devices with their start and end apart: 4, of which 2 were waited for; matrix products, arithmetic and copies ran while one was open for 0% of the time, Pallas kernels for 15%

profile of v5, /device:TPU:0, one launch (start us, length us, event | category | flops | bytes accessed | tf_op | source)
XLA Modules:
  0.0 32.5 jit_solution(5725270308279184605)
XLA Ops:
  0.0 0.0 copy-start.4
  0.0 0.0 copy-start.5
  0.0 0.0 copy-start.6
  0.0 3.7 %shard_map.100 = (bf16[288,1728]{1,0:T(8,128)(2,1)S(1)}, bf16[6,96,256]{2,1,0:T(8,128)(2,1)S(1)}, f32[6,96,384]{2,1,0:T(8,128)S(1)}, bf16[4,192,4,128]{3,2,1,0:T(4,128)(2,1)S(1)}, bf16[12,16,128]{2,1,0:T(8,128)(2,1)S(1)}) custom-call(s32[16]{0:T(128)} %clip_hbm.1, bf16[4,192,4,128]{3,2,1,0:T(4,128)(2,1)} %lat_hbm.1, bf16[3,3,3,96,192]{4,3,2,1,0:T(8,128)(2,1)} %weight_hbm.1, ...), custom_call_target="tpu_custom_call" | custom-call | flops 1019215872 | bytes 4793152 | tf_op jit(solution)/shard_map/pallas_call | solution.py:259
  3.7 4.9 %collective-permute-start.1 = (bf16[6,96,256]{2,1,0:T(8,128)(2,1)S(1)}, bf16[6,96,256]{2,1,0:T(8,128)(2,1)S(1)}, u32[]{:S(2)}, u32[]{:S(2)}) collective-permute-start(bf16[6,96,256]{2,1,0:T(8,128)(2,1)S(1)} %get-tuple-element.26), channel_id=1, source_target_pairs={{0,1},{1,2},{2,3},{3,4},{4,5},{5,6},{6,7},{8,9},{9,10},{10,11},{11... | collective-permute-start | bytes 884744 | tf_op jit(solution)/shard_map/ppermute | solution.py:272
  8.6 0.0 copy-done.4
  8.6 0.0 copy-done.5
  8.6 0.0 copy-done.6
  8.6 1.8 %shard_map.101 = (f32[4,96,256]{2,1,0:T(8,128)S(1)}, bf16[4,96,384]{2,1,0:T(8,128)(2,1)S(1)}, bf16[2304,256]{1,0:T(8,128)(2,1)S(1)}, f32[2,96,128]{2,1,0:T(8,128)S(1)}) custom-call(bf16[12,16,128]{2,1,0:T(8,128)(2,1)S(1)} %get-tuple-element.18.keep_ref, bf16[4,192,4,128]{3,2,1,0:T(4,128)(2,1)S(1)} %get-tuple-element.19.lat_ref, f32[1,192]{1,0:T(1,128)S(1)} %bitcast.8, ...), custom_call_target="tpu_custom_call" | custom-call | flops 1019215872 | bytes 4683264 | tf_op jit(solution)/shard_map/pallas_call | solution.py:259
  10.4 0.0 copy-start
  10.4 4.4 %collective-permute-done.1.got_ref = bf16[6,96,256]{2,1,0:T(8,128)(2,1)S(1)} collective-permute-done((bf16[6,96,256]{2,1,0:T(8,128)(2,1)S(1)}, bf16[6,96,256]{2,1,0:T(8,128)(2,1)S(1)}, u32[]{:S(2)}, u32[]{:S(2)}) %collective-permute-start.1) | collective-permute-done | bytes 294944 | tf_op jit(solution)/shard_map/ppermute | solution.py:272
  14.8 0.1 shard_map.103.mine_ref
  15.0 1.3 %collective-permute-start.2 = (bf16[4,96,256]{2,1,0:T(8,128)(2,1)S(1)}, bf16[4,96,256]{2,1,0:T(8,128)(2,1)S(1)}, u32[]{:S(2)}, u32[]{:S(2)}) collective-permute-start(bf16[4,96,256]{2,1,0:T(8,128)(2,1)S(1)} %shard_map.103.mine_ref), channel_id=1, source_target_pairs={{0,8},{8,16},{16,24},{1,9},{9,17},{17,25},{2,10},{10,18},{18,26},{... | collective-permute-start | bytes 589832 | tf_op jit(solution)/shard_map/ppermute | solution.py:272
  16.3 4.1 %collective-permute-start = (bf16[4,96,384]{2,1,0:T(8,128)(2,1)S(1)}, bf16[4,96,384]{2,1,0:T(8,128)(2,1)S(1)}, u32[]{:S(2)}, u32[]{:S(2)}) collective-permute-start(bf16[4,96,384]{2,1,0:T(8,128)(2,1)S(1)} %get-tuple-element.24.mine_ref), channel_id=1, source_target_pairs={{0,8},{8,16},{16,24},{1,9},{9,17},{17,25},{2,10},{10,18},{18,26},{... | collective-permute-start | bytes 884744 | tf_op jit(solution)/shard_map/ppermute | solution.py:272
  20.4 0.0 copy-done
  20.4 0.5 %shard_map.102 = (f32[2,96,640]{2,1,0:T(8,128)S(1)}, bf16[288,864]{1,0:T(8,128)(2,1)S(1)}) custom-call(bf16[12,16,128]{2,1,0:T(8,128)(2,1)S(1)} %get-tuple-element.18.keep_ref, bf16[2304,256]{1,0:T(8,128)(2,1)S(1)} %get-tuple-element.22.xs_ref, bf16[288,1728]{1,0:T(8,128)(2,1)S(1)} %get-tuple-element.20.wt_ref, ...), custom_call_target="tpu_custom_call" | custom-call | flops 509607936 | bytes 4595712 | tf_op jit(solution)/shard_map/pallas_call | solution.py:259
  20.9 0.0 copy-start.1
  20.9 0.0 copy-start.2
  20.9 0.0 copy-start.3
  21.0 0.0 collective-permute-done.2.before_ref
  21.0 1.0 %shard_map.104 = (bf16[4,96,256]{2,1,0:T(8,128)(2,1)S(1)}, f32[4,96,256]{2,1,0:T(8,128)S(1)}) custom-call(bf16[12,16,128]{2,1,0:T(8,128)(2,1)S(1)} %get-tuple-element.18.keep_ref, f32[2,96,640]{2,1,0:T(8,128)S(1)} %get-tuple-element.23.head_ref, bf16[6,96,256]{2,1,0:T(8,128)(2,1)S(1)} %collective-permute-done.1.got_ref, ...), custom_call_target="tpu_custom_call" | custom-call | flops 509607936 | bytes 2414592 | tf_op jit(solution)/shard_map/pallas_call | solution.py:259
  22.0 1.3 %collective-permute-start.3 = (bf16[4,96,256]{2,1,0:T(8,128)(2,1)S(1)}, bf16[4,96,256]{2,1,0:T(8,128)(2,1)S(1)}, u32[]{:S(2)}, u32[]{:S(2)}) collective-permute-start(bf16[4,96,256]{2,1,0:T(8,128)(2,1)S(1)} %get-tuple-element.30), channel_id=1, source_target_pairs={{1,0},{2,1},{3,2},{4,3},{5,4},{6,5},{7,6},{9,8},{10,9},{11,10},{12... | collective-permute-start | bytes 589832 | tf_op jit(solution)/shard_map/ppermute | solution.py:272
  23.3 0.0 collective-permute-done.before_ref
  23.3 0.0 copy-done.1
  23.3 0.0 copy-done.2
  23.3 0.0 copy-done.3
  23.3 1.7 %shard_map.105.total_ref = f32[4,96,512]{2,1,0:T(8,128)S(1)} custom-call(bf16[12,16,128]{2,1,0:T(8,128)(2,1)S(1)} %get-tuple-element.18.keep_ref, f32[2,96,640]{2,1,0:T(8,128)S(1)} %get-tuple-element.23.head_ref, bf16[4,96,384]{2,1,0:T(8,128)(2,1)S(1)} %get-tuple-element.24.mine_ref, bf16[4,96,384]{2,1,0:T(8,128)(2,1)S(1)} %collective-permute-done.before_ref, ...), custom_call_target="tpu_custom_call" | custom-call | flops 764411904 | bytes 3730176 | tf_op jit(solution)/shard_map/pallas_call | solution.py:259
  25.1 6.5 %collective-permute-done.3.below_ref = bf16[4,96,256]{2,1,0:T(8,128)(2,1)S(1)} collective-permute-done((bf16[4,96,256]{2,1,0:T(8,128)(2,1)S(1)}, bf16[4,96,256]{2,1,0:T(8,128)(2,1)S(1)}, u32[]{:S(2)}, u32[]{:S(2)}) %collective-permute-start.3) | collective-permute-done | bytes 196640 | tf_op jit(solution)/shard_map/ppermute | solution.py:272
  31.5 1.0 %shard_map.106 = bf16[4,96,4,128]{3,2,1,0:T(4,128)(2,1)} custom-call(f32[4,96,512]{2,1,0:T(8,128)S(1)} %shard_map.105.total_ref, bf16[4,96,256]{2,1,0:T(8,128)(2,1)S(1)} %collective-permute-done.3.below_ref), custom_call_target="tpu_custom_call" | custom-call | flops 1000 | bytes 1376256 | tf_op jit(solution)/shard_map/pallas_call | solution.py:259
Async XLA Ops:
  0.0 8.6 %copy-start.4 = (f32[192]{0:T(256)S(1)}, f32[192]{0:T(256)}, u32[]{:S(2)}) copy-start(f32[192]{0:T(256)} %param.12) | copy-start | bytes 2308
  0.0 8.6 %copy-start.5 = (f32[96]{0:T(128)S(1)}, f32[96]{0:T(128)}, u32[]{:S(2)}) copy-start(f32[96]{0:T(128)} %param.14) | copy-start | bytes 1156
  0.0 8.6 %copy-start.6 = (f32[96]{0:T(128)S(1)}, f32[96]{0:T(128)}, u32[]{:S(2)}) copy-start(f32[96]{0:T(128)} %param.15) | copy-start | bytes 1156
  3.7 11.2 %collective-permute-start.1 = (bf16[6,96,256]{2,1,0:T(8,128)(2,1)S(1)}, bf16[6,96,256]{2,1,0:T(8,128)(2,1)S(1)}, u32[]{:S(2)}, u32[]{:S(2)}) collective-permute-start(bf16[6,96,256]{2,1,0:T(8,128)(2,1)S(1)} %get-tuple-element.26), channel_id=1, source_target_pairs={{0,1},{1,2},{2,3},{3,4},{4,5},{5,6},{6,7},{8,9},{9,10},{10,11},{11... | collective-permute-start | bytes 884744 | tf_op jit(solution)/shard_map/ppermute | solution.py:272
  10.4 10.0 %copy-start = (bf16[3,3,3,96,96]{4,3,2,1,0:T(8,128)(2,1)S(1)}, bf16[3,3,3,96,96]{4,3,2,1,0:T(8,128)(2,1)}, u32[]{:S(2)}) copy-start(bf16[3,3,3,96,96]{4,3,2,1,0:T(8,128)(2,1)} %weight_ref.1) | copy-start | bytes 1492996
  15.0 6.0 %collective-permute-start.2 = (bf16[4,96,256]{2,1,0:T(8,128)(2,1)S(1)}, bf16[4,96,256]{2,1,0:T(8,128)(2,1)S(1)}, u32[]{:S(2)}, u32[]{:S(2)}) collective-permute-start(bf16[4,96,256]{2,1,0:T(8,128)(2,1)S(1)} %shard_map.103.mine_ref), channel_id=1, source_target_pairs={{0,8},{8,16},{16,24},{1,9},{9,17},{17,25},{2,10},{10,18},{18,26},{... | collective-permute-start | bytes 589832 | tf_op jit(solution)/shard_map/ppermute | solution.py:272
  16.3 7.0 %collective-permute-start = (bf16[4,96,384]{2,1,0:T(8,128)(2,1)S(1)}, bf16[4,96,384]{2,1,0:T(8,128)(2,1)S(1)}, u32[]{:S(2)}, u32[]{:S(2)}) collective-permute-start(bf16[4,96,384]{2,1,0:T(8,128)(2,1)S(1)} %get-tuple-element.24.mine_ref), channel_id=1, source_target_pairs={{0,8},{8,16},{16,24},{1,9},{9,17},{17,25},{2,10},{10,18},{18,26},{... | collective-permute-start | bytes 884744 | tf_op jit(solution)/shard_map/ppermute | solution.py:272
  20.9 2.4 %copy-start.1 = (bf16[96,192]{1,0:T(8,128)(2,1)S(1)}, bf16[96,192]{1,0:T(8,128)(2,1)}, u32[]{:S(2)}) copy-start(bf16[96,192]{1,0:T(8,128)(2,1)} %skip_ref.1) | copy-start | bytes 110596
  20.9 2.4 %copy-start.2 = (f32[96]{0:T(128)S(1)}, f32[96]{0:T(128)}, u32[]{:S(2)}) copy-start(f32[96]{0:T(128)} %param.17) | copy-start | bytes 1156
  20.9 2.4 %copy-start.3 = (f32[96]{0:T(128)S(1)}, f32[96]{0:T(128)}, u32[]{:S(2)}) copy-start(f32[96]{0:T(128)} %param.19) | copy-start | bytes 1156
  22.0 9.6 %collective-permute-start.3 = (bf16[4,96,256]{2,1,0:T(8,128)(2,1)S(1)}, bf16[4,96,256]{2,1,0:T(8,128)(2,1)S(1)}, u32[]{:S(2)}, u32[]{:S(2)}) collective-permute-start(bf16[4,96,256]{2,1,0:T(8,128)(2,1)S(1)} %get-tuple-element.30), channel_id=1, source_target_pairs={{1,0},{2,1},{3,2},{4,3},{5,4},{6,5},{7,6},{9,8},{10,9},{11,10},{12... | collective-permute-start | bytes 589832 | tf_op jit(solution)/shard_map/ppermute | solution.py:272
